TPU v7x, 32 devices: a whole 2x2x4 slice. The times are simulated.
32 devices in a mesh: space: 8 (over z, y), band: 4 (over x, core).
Axes of the slice: x: 2, y: 2, z: 4, core: 2. Of those that a mesh axis runs over, the one named last changes fastest.
Arguments:
- columns: float32 [16, 48, 32, 128], P('band', 'space'), may hold values from -6 to 6
- potential: float32 [48, 32, 128], P('space'), may hold values from -1 to 3
- orbitals: float32 [512, 48, 32, 128], P('band', 'space'), may hold values from -0.0546875 to 0.0546875
Outputs:
- projected: float32 [16, 48, 32, 128], P('band', 'space')
- correlation: float32 [512, 16], P('band')
All inputs are finite; a program needn't handle non-finite values.
Results may differ from a plain program's by a relative error of at most 0.00011.
Values sent between devices are 32-bit elements; how exact they have to be, the bound alone decides.
No kernel may reach another device: no remote copies, remote signals or barrier semaphores. Data moves between devices by JAX's collectives and lax.ppermute only.
A program may use at most 128 MiB of HBM per device.

v0:
```python
import jax
import jax.numpy as jnp
from jax import lax
from jax.sharding import PartitionSpec as P

COEFFS = (
    -5369.0 / 1800.0,
    12.0 / 7.0,
    -15.0 / 56.0,
    10.0 / 189.0,
    -1.0 / 112.0,
    2.0 / 1925.0,
    -1.0 / 16632.0,
)


def padded_2(array, sides, width):
    for axis, dim in sides:
        size, length = (lax.axis_size(axis), array.shape[dim])
        up = [(i, (i + 1) % size) for i in range(size)]
        down = [(j, i) for i, j in up]
        last = lax.slice_in_dim(array, length - width, length, axis=dim)
        first = lax.slice_in_dim(array, 0, width, axis=dim)
        before = lax.ppermute(last, axis, up)
        after = lax.ppermute(first, axis, down)
        array = jnp.concatenate([before, array, after], axis=dim)
    return array


def hamiltonian(values, potential):
    padded = padded_2(values, (("space", 1),), 6)
    planes = values.shape[1]
    laplace = 3.0 * COEFFS[0] * values
    for offset in range(1, 7):
        along = (
            padded[:, 6 + offset : 6 + offset + planes]
            + padded[:, 6 - offset : 6 - offset + planes]
        )
        along = along + jnp.roll(values, offset, 2) + jnp.roll(values, -offset, 2)
        along = along + jnp.roll(values, offset, 3) + jnp.roll(values, -offset, 3)
        laplace = laplace + COEFFS[offset] * along
    return -0.5 * laplace + potential[None] * values


def shards(columns, potential, orbitals):
    applied = hamiltonian(columns, potential)
    orb_local = orbitals.shape[0]
    col_local = applied.shape[0]
    psi_flat = orbitals.reshape(orb_local, -1)
    piece = lax.all_gather(applied, "band", axis=0, tiled=True)
    partial_correlation = jnp.einsum(
        "oc,kc->ok", psi_flat, piece.reshape(piece.shape[0], -1), precision=lax.Precision.HIGHEST
    )
    correlation = lax.psum(partial_correlation, "space")
    removed = jnp.einsum("ok,oc->kc", correlation, psi_flat, precision=lax.Precision.HIGHEST)
    removed_all = lax.psum_scatter(
        removed.reshape((col_local * lax.axis_size("band"),) + applied.shape[1:]),
        "band",
        scatter_dimension=0,
        tiled=True,
    )
    projected = applied - removed_all
    return (projected, correlation)


def solution(mesh):
    placed = (
        P("band", "space", None, None),
        P("space", None, None),
        P("band", "space", None, None),
    )
    return jax.shard_map(
        shards,
        mesh=mesh,
        in_specs=placed,
        out_specs=(P("band", "space", None, None), P("band", None)),
        check_vma=False,
    )
```

profile of v0, /device:TPU:0, one launch (start us, length us, event | category | flops | bytes accessed | tf_op | source)
XLA Modules:
  0.0 155.2 jit_solution(5152359355266835999)
XLA Ops:
  7.2 3.0 %collective-permute-start.1 = (f32[4,6,32,128]{3,2,1,0:T(8,128)}, f32[4,6,32,128]{3,2,1,0:T(8,128)S(1)}, u32[]{:S(2)}, u32[]{:S(2)}) collective-permute-start(f32[4,6,32,128]{3,2,1,0:T(8,128)} %param.3), channel_id=1, source_target_pairs={{0,4},{4,8},{8,12},{12,16},{16,20},{20,24},{24,28},{28,0},{1,5},{5... | collective-permute-start | bytes 1179656 | tf_op jit(solution)/shard_map/ppermute | solution.py:24
  10.3 3.1 %collective-permute-start = (f32[4,6,32,128]{3,2,1,0:T(8,128)}, f32[4,6,32,128]{3,2,1,0:T(8,128)S(1)}, u32[]{:S(2)}, u32[]{:S(2)}) collective-permute-start(f32[4,6,32,128]{3,2,1,0:T(8,128)} %param.3), channel_id=1, source_target_pairs={{4,0},{8,4},{12,8},{16,12},{20,16},{24,20},{28,24},{0,28},{5,1},{9... | collective-permute-start | bytes 1179656 | tf_op jit(solution)/shard_map/ppermute | solution.py:25
  13.4 1.3 fusion.69
  14.6 1.4 fusion.67
  16.0 1.4 fusion.68
  17.4 1.3 fusion.65
  18.6 1.4 fusion.63
  20.0 1.4 fusion.64
  21.4 1.3 fusion.61
  22.6 1.0 fusion.62
  23.6 1.4 fusion.59
  25.0 0.2 fusion.60
  25.2 0.1 fusion.57
  25.3 0.2 fusion.55
  25.4 0.2 fusion.56
  25.7 0.2 fusion.51
  25.9 0.2 fusion.52
  26.2 0.2 fusion.47
  26.4 0.2 fusion.48
  26.6 0.8 collective-permute-done.1
  27.4 0.1 constant_dynamic-update-slice_fusion.1
  27.5 2.0 %collective-permute-done = f32[4,6,32,128]{3,2,1,0:T(8,128)S(1)} collective-permute-done((f32[4,6,32,128]{3,2,1,0:T(8,128)}, f32[4,6,32,128]{3,2,1,0:T(8,128)S(1)}, u32[]{:S(2)}, u32[]{:S(2)}) %collective-permute-start) | collective-permute-done | bytes 393248 | tf_op jit(solution)/shard_map/ppermute | solution.py:25
  29.5 3.8 %fusion.16 = f32[4,6,32,128]{3,2,1,0:T(8,128)} fusion(f32[4,12,32,128]{3,2,1,0:T(8,128)S(1)} %get-tuple-element.53, f32[4,12,32,128]{3,2,1,0:T(8,128)S(1)} %constant_dynamic-update-slice_fusion, f32[4,6,31,128]{3,2,1,0:T(8,128)S(1)} %get-tuple-element.49, f32[4,6,1,128]{3,2,1,0:T(1,128)S(1)} %get-tuple-element.51, ...), kind=kLoop, calls=%fused_computation.14 | loop fusion | flops 6881280 | bytes 15040512 | tf_op jit(solution)/shard_map/add | solution.py:42
  33.3 0.2 reduce-scatter.2.cloned.1.call-start
  33.6 18.9 %copy.78 = f32[16,8,192,128]{3,1,2,0:T(8,128)} copy(f32[16,8,192,128]{3,2,1,0:T(8,128)} %bitcast.21) | data formatting | bytes 25165824
  52.5 12.6 %copy.64 = f32[24576,128]{1,0:T(8,128)} copy(f32[24576,128]{0,1:T(8,128)} %bitcast.23) | data formatting | bytes 25165824 | tf_op jit(solution)/shard_map/ok,oc->kc/dot_general | solution.py:55
  65.1 20.7 %fusion.3 = f32[128,16]{0,1:T(8,128)S(1)} fusion(f32[128,6,32,128]{3,2,1,0:T(8,128)} %param.5, f32[16,6,32,128]{3,2,1,0:T(8,128)} %all-gather.2.cloned.1.call-done), kind=kOutput, calls=%fused_computation.4 | convolution fusion | flops 603979776 | bytes 14163968 | tf_op jit(solution)/shard_map/oc,kc->ok/dot_general | solution.py:51
  85.8 21.0 %psum.7 = f32[128,16]{0,1:T(8,128)S(1)} all-reduce(f32[128,16]{0,1:T(8,128)S(1)} %fusion.3), channel_id=1, replica_groups=mesh['space'=8,'band'=4] {'space'}, use_global_device_ids=true, to_apply=%region_0.1 | all-reduce | flops 2048 | bytes 16384 | tf_op jit(solution)/shard_map/psum | solution.py:54
  106.7 12.7 %fusion.45 = f32[16,6,32,128]{3,0,2,1:T(8,128)S(1)} fusion(f32[6,32,128,128]{3,2,1,0:T(8,128)} %bitcast.22, f32[128,16]{0,1:T(8,128)S(1)} %psum.7), kind=kOutput, calls=%fused_computation.52 | convolution fusion | flops 603979776 | bytes 14163968 | tf_op jit(solution)/shard_map/ok,oc->kc/dot_general | solution.py:55
  119.5 1.7 %copy.65 = f32[16,6,32,128]{3,2,1,0:T(8,128)} copy(f32[16,6,32,128]{3,0,2,1:T(8,128)S(1)} %fusion.45) | data formatting | bytes 3145728 | tf_op jit(solution)/shard_map/ok,oc->kc/dot_general | solution.py:55
  121.2 25.4 %reduce-scatter.2.cloned.1.call-done = f32[4,6,32,128]{3,2,1,0:T(8,128)} async-done(((f32[16,6,32,128]{3,2,1,0:T(8,128)}), f32[4,6,32,128]{3,2,1,0:T(8,128)}) %reduce-scatter.2.cloned.1.call-update) | async-done | bytes 393232 | tf_op jit(solution)/shard_map/reduce_scatter | solution.py:56
  146.6 1.8 %sub.3 = f32[4,6,32,128]{3,2,1,0:T(8,128)} subtract(f32[4,6,32,128]{3,2,1,0:T(8,128)S(1)} %copy-done.1, f32[4,6,32,128]{3,2,1,0:T(8,128)} %reduce-scatter.2.cloned.1.call-done) | non-fusion elementwise | flops 98304 | bytes 1179648 | tf_op jit(solution)/shard_map/sub | solution.py:62
  (21 shorter events, 0.4 us)
Async XLA Ops:
  7.2 17.8 %copy-start = (f32[4,6,32,128]{3,2,1,0:T(8,128)S(1)}, f32[4,6,32,128]{3,2,1,0:T(8,128)}, u32[]{:S(2)}) copy-start(f32[4,6,32,128]{3,2,1,0:T(8,128)} %param.3) | copy-start | bytes 1179652
  7.2 57.9 %all-gather.2.cloned.1.call-start = ((), (), s32[]{:S(2)}) async-start(), calls=%async_computation.1 | async-start | bytes 1966080 | tf_op jit(solution)/shard_map/all_gather | solution.py:50
  7.2 20.2 %collective-permute-start.1 = (f32[4,6,32,128]{3,2,1,0:T(8,128)}, f32[4,6,32,128]{3,2,1,0:T(8,128)S(1)}, u32[]{:S(2)}, u32[]{:S(2)}) collective-permute-start(f32[4,6,32,128]{3,2,1,0:T(8,128)} %param.3), channel_id=1, source_target_pairs={{0,4},{4,8},{8,12},{12,16},{16,20},{20,24},{24,28},{28,0},{1,5},{5... | collective-permute-start | bytes 1179656 | tf_op jit(solution)/shard_map/ppermute | solution.py:24
  10.3 19.2 %collective-permute-start = (f32[4,6,32,128]{3,2,1,0:T(8,128)}, f32[4,6,32,128]{3,2,1,0:T(8,128)S(1)}, u32[]{:S(2)}, u32[]{:S(2)}) collective-permute-start(f32[4,6,32,128]{3,2,1,0:T(8,128)} %param.3), channel_id=1, source_target_pairs={{4,0},{8,4},{12,8},{16,12},{20,16},{24,20},{28,24},{0,28},{5,1},{9... | collective-permute-start | bytes 1179656 | tf_op jit(solution)/shard_map/ppermute | solution.py:25
  20.0 9.5 %copy-start.2 = (f32[6,32,128]{2,1,0:T(8,128)S(1)}, f32[6,32,128]{2,1,0:T(8,128)}, u32[]{:S(2)}) copy-start(f32[6,32,128]{2,1,0:T(8,128)} %param.4) | copy-start | bytes 294916
  33.3 113.2 %reduce-scatter.2.cloned.1.call-start = ((), (), s32[]{:S(2)}) async-start(), calls=%async_computation.2 | async-start | bytes 1966080 | tf_op jit(solution)/shard_map/reduce_scatter | solution.py:56
  85.7 60.8 %copy-start.1 = (f32[4,6,32,128]{3,2,1,0:T(8,128)S(1)}, f32[4,6,32,128]{3,2,1,0:T(8,128)}, u32[]{:S(2)}) copy-start(f32[4,6,32,128]{3,2,1,0:T(8,128)} %fusion.16) | copy-start | bytes 1179652
  106.7 41.6 %copy-start.3 = (f32[128,16]{0,1:T(8,128)}, f32[128,16]{0,1:T(8,128)S(1)}, u32[]{:S(2)}) copy-start(f32[128,16]{0,1:T(8,128)S(1)} %psum.7) | copy-start | bytes 24580
Sparse Core Ops, SparseCore 0:
  33.5 19.7 all-gather.1
  121.3 25.2 reduce-scatter.1
where the time goes:
time: 156 us; the launch traced here: 155 us
  local copies, waits for them, and re-layouts  46.5 us (30%)
  matrix products  33.4 us (21%)
  waiting for transfers between devices  28.2 us (18%)
  blocking collectives  21 us (13%)
  between operations  14.2 us (9%)
  starting transfers between devices  6.41 us (4%)
  other arithmetic  5.59 us (4%)
    reduce_scatter x1, waiting for transfers between devices, shards(): lax.psum_scatter(removed.reshape((col_local * lax.axis_size('band'),) + a...  25.4 us
    psum x1, blocking collectives, shards(): correlation = lax.psum(partial_correlation, 'space')  21 us
    dot_general x1, matrix products, shards(): jnp.einsum('oc,kc->ok', psi_flat, piece.reshape(piece.shape[0], -1), prec...  20.7 us
    unnamed x11, local copies, waits for them, and re-layouts  19 us
    dot_general x2, local copies, waits for them, and re-layouts, shards(): jnp.einsum('ok,oc->kc', correlation, psi_flat, precision=lax.Precision.HI...  14.3 us
    dot_general x1, matrix products, shards(): jnp.einsum('ok,oc->kc', correlation, psi_flat, precision=lax.Precision.HI...  12.7 us
    slice x12, local copies, waits for them, and re-layouts, hamiltonian(): along = along + jnp.roll(values, offset, 3) + jnp.roll(values, -offset, 3)  8.09 us
    slice x12, local copies, waits for them, and re-layouts, hamiltonian(): along = along + jnp.roll(values, offset, 2) + jnp.roll(values, -offset, 2)  5.05 us
  transfers between devices with their start and end apart: 4, of which 3 were waited for; matrix products, arithmetic and copies ran while one was open for 29% of the time, Pallas kernels for 0%

commit v1 on v0

v1 whole, which is shorter than its diff:
```python
import functools

import jax
import jax.numpy as jnp
from jax import lax
from jax.experimental import pallas as pl
from jax.experimental.pallas import tpu as pltpu
from jax.sharding import PartitionSpec as P

COEFFS = (
    -5369.0 / 1800.0,
    12.0 / 7.0,
    -15.0 / 56.0,
    10.0 / 189.0,
    -1.0 / 112.0,
    2.0 / 1925.0,
    -1.0 / 16632.0,
)
WIDTH = 6
SUB = 8
F32 = jnp.float32
BF16 = jnp.bfloat16
VMEM = pl.BlockSpec(memory_space=pltpu.VMEM)
LIMIT = 24 << 20


def near(x):
    return pltpu.with_memory_space_constraint(x, pltpu.VMEM)


def params(limit=LIMIT):
    return pltpu.CompilerParams(vmem_limit_bytes=limit)


def halves(x):
    hi = x.astype(BF16)
    lo = (x - hi.astype(F32)).astype(BF16)
    return hi, lo


def split_kernel(psi_ref, hi_ref, lo_ref):
    orbs = psi_ref.shape[0]
    lanes = psi_ref.shape[3]
    for g in range(psi_ref.shape[2] // SUB):
        x = psi_ref[:, 0, g * SUB : (g + 1) * SUB, :].reshape(orbs * SUB, lanes)
        hi, lo = halves(x)
        hi_ref[pl.program_id(0), :, g * lanes : (g + 1) * lanes] = hi
        lo_ref[pl.program_id(0), :, g * lanes : (g + 1) * lanes] = lo


def split(orbitals):
    orbs, planes, ny, nx = orbitals.shape
    rows = 2 * SUB
    per = ny // rows
    shape = pltpu.VMEM((planes * per, orbs * SUB, 2 * nx), BF16)
    return pl.pallas_call(
        split_kernel,
        grid=(planes * per,),
        in_specs=[pl.BlockSpec((orbs, 1, rows, nx), lambda p: (0, p // per, p % per, 0))],
        out_specs=[VMEM, VMEM],
        out_shape=[shape, shape],
        compiler_params=params(),
        cost_estimate=pl.CostEstimate(
            flops=4 * orbitals.size, bytes_accessed=8 * orbitals.size, transcendentals=0
        ),
        name="split",
    )(orbitals)


def local_kernel(v_ref, pot_ref, out_ref):
    cols, planes, _, _ = v_ref.shape

    def column(c, carry):
        for z in range(planes):
            v = v_ref[c, z]
            total = (pot_ref[z] - 1.5 * COEFFS[0]) * v
            for k in range(1, WIDTH + 1):
                along = pltpu.roll(v, k, 1) + pltpu.roll(v, v.shape[1] - k, 1)
                along = along + pltpu.roll(v, k, 0) + pltpu.roll(v, v.shape[0] - k, 0)
                if z + k < planes:
                    along = along + v_ref[c, z + k]
                if z - k >= 0:
                    along = along + v_ref[c, z - k]
                total = total - (0.5 * COEFFS[k]) * along
            out_ref[c, z] = total
        return carry

    lax.fori_loop(0, cols, column, 0)


def halo_kernel(own_ref, before_ref, after_ref, out_ref):
    cols, planes, _, _ = own_ref.shape

    def column(c, carry):
        for z in range(planes):
            total = own_ref[c, z]
            for k in range(1, WIDTH + 1):
                if z - k < 0:
                    total = total - (0.5 * COEFFS[k]) * before_ref[c, WIDTH + z - k]
                if z + k >= planes:
                    total = total - (0.5 * COEFFS[k]) * after_ref[c, z + k - planes]
            out_ref[c, z] = total
        return carry

    lax.fori_loop(0, cols, column, 0)


def rows_of(refs, z, y):
    return jnp.concatenate(
        [
            jnp.concatenate(
                [
                    ref[:, z, y + g * SUB : y + (g + 1) * SUB, :].reshape(
                        ref.shape[0] * SUB, ref.shape[3]
                    )
                    for ref in refs
                ],
                axis=0,
            )
            for g in range(2)
        ],
        axis=1,
    )


def corr_kernel(count, hi_ref, lo_ref, *refs):
    blocks, out_ref = refs[:count], refs[count]
    big_ref, small_ref = refs[count + 1 :]
    pairs, rows, _ = hi_ref.shape
    planes, ny = blocks[0].shape[1:3]
    per = ny // (2 * SUB)
    width = sum(b.shape[0] for b in blocks) * SUB
    contract = (((1,), (1,)), ((), ()))
    for p in range(pairs):
        w_hi, w_lo = halves(rows_of(blocks, p // per, (p % per) * 2 * SUB))
        both = jnp.concatenate([w_hi, w_lo], axis=0)
        big = lax.dot_general(hi_ref[p], both, contract, preferred_element_type=F32)
        small = lax.dot_general(lo_ref[p], w_hi, contract, preferred_element_type=F32)
        if p == 0:
            big_ref[...] = big
            small_ref[...] = small
        else:
            big_ref[...] += big
            small_ref[...] += small
    total = big_ref[:, :width] + big_ref[:, width:] + small_ref[...]
    total = total.reshape(rows // SUB, SUB, width)
    at = lax.broadcasted_iota(jnp.int32, total.shape, 1)
    lane = lax.broadcasted_iota(jnp.int32, total.shape, 2)
    diag = jnp.sum(jnp.where(lane % SUB == at, total, 0.0), axis=1)
    cols = width // SUB
    pick = lax.broadcasted_iota(jnp.int32, (cols, width), 1) // SUB
    pick = pick == lax.broadcasted_iota(jnp.int32, (cols, width), 0)
    out_ref[...] = lax.dot_general(
        pick.astype(F32),
        diag,
        contract,
        precision=lax.Precision.HIGHEST,
        preferred_element_type=F32,
    )


def correlate(hi, lo, blocks):
    cols = sum(b.shape[0] for b in blocks)
    orbs = hi.shape[1] // SUB
    return pl.pallas_call(
        functools.partial(corr_kernel, len(blocks)),
        in_specs=[VMEM] * (2 + len(blocks)),
        out_specs=VMEM,
        out_shape=pltpu.VMEM((cols, orbs), F32),
        compiler_params=params(),
        scratch_shapes=[
            pltpu.VMEM((orbs * SUB, 2 * cols * SUB), F32),
            pltpu.VMEM((orbs * SUB, cols * SUB), F32),
        ],
        name="corr",
    )(near(hi), near(lo), *map(near, blocks))


def add_kernel(*refs):
    total = refs[0][...]
    for ref in refs[1:-1]:
        total = total + ref[...]
    refs[-1][...] = total


def add(*parts):
    return pl.pallas_call(
        add_kernel,
        in_specs=[VMEM] * len(parts),
        out_specs=VMEM,
        out_shape=pltpu.VMEM(parts[0].shape, F32),
        compiler_params=params(),
        name="add",
    )(*map(near, parts))


def remove_kernel(order, count, me_ref, *refs):
    parts = refs[:count]
    hi_ref, lo_ref, out_ref, keep_ref, send_ref = refs[count:]
    cols, orbs = out_ref.shape
    pairs, rows, wide = hi_ref.shape
    nx = wide // 2
    per = keep_ref.shape[2] // (2 * SUB)
    half = keep_ref.shape[0]
    corr = parts[0][...]
    for part in parts[1:]:
        corr = corr + part[...]
    step = cols // len(order)
    pieces = [None] * len(order)
    for at, r in enumerate(order):
        pieces[r] = corr[at * step : (at + 1) * step]
    mask = 1
    while mask < len(order):
        swap = (me_ref[0] & mask) != 0
        pieces = [jnp.where(swap, pieces[r ^ mask], pieces[r]) for r in range(len(order))]
        mask *= 2
    out_ref[...] = jnp.concatenate(pieces, axis=0)

    spread = lax.broadcasted_iota(jnp.int32, (orbs, rows), 1) // SUB
    spread = (spread == lax.broadcasted_iota(jnp.int32, (orbs, rows), 0)).astype(BF16)
    tall = jnp.broadcast_to(corr[:, None, :], (cols, SUB, orbs)).reshape(cols * SUB, orbs)
    at = lax.broadcasted_iota(jnp.int32, (cols * SUB, rows), 0) % SUB
    same = at == lax.broadcasted_iota(jnp.int32, (cols * SUB, rows), 1) % SUB
    c_hi, c_lo = [
        jnp.where(same, jnp.dot(part, spread, preferred_element_type=F32), 0.0).astype(BF16)
        for part in halves(tall)
    ]
    both = jnp.concatenate([c_hi, c_lo], axis=0)
    height = cols * SUB
    for p in range(pairs):
        big = jnp.dot(both, hi_ref[p], preferred_element_type=F32)
        small = jnp.dot(c_hi, lo_ref[p], preferred_element_type=F32)
        total = big[:height] + big[height:] + small
        z, y = p // per, (p % per) * 2 * SUB
        for g in range(2):
            part = total[:, g * nx : (g + 1) * nx].reshape(cols, SUB, nx)
            keep_ref[:, z, y + g * SUB : y + (g + 1) * SUB, :] = part[:half]
            send_ref[:, z, y + g * SUB : y + (g + 1) * SUB, :] = part[half:]


def remove(order, me, parts, hi, lo, planes, ny, nx):
    cols, orbs = parts[0].shape
    part = pltpu.VMEM((cols // 2, planes, ny, nx), F32)
    return pl.pallas_call(
        functools.partial(remove_kernel, order, len(parts)),
        in_specs=[pl.BlockSpec(memory_space=pltpu.SMEM)] + [VMEM] * (len(parts) + 2),
        out_specs=[VMEM] * 3,
        out_shape=[pltpu.VMEM((cols, orbs), F32), part, part],
        compiler_params=params(),
        name="remove",
    )(me, *map(near, parts), near(hi), near(lo))


def swap(x, axis, mask):
    size = lax.axis_size(axis)
    return lax.ppermute(x, axis, [(i, i ^ mask) for i in range(size)])


def shards(columns, potential, orbitals):
    cols, planes, ny, nx = columns.shape
    space, band = lax.axis_size("space"), lax.axis_size("band")
    up = [(i, (i + 1) % space) for i in range(space)]
    down = [(j, i) for i, j in up]
    before = lax.ppermute(columns[:, planes - WIDTH :], "space", up)
    after = lax.ppermute(columns[:, :WIDTH], "space", down)
    me = lax.axis_index("band").astype(jnp.int32).reshape(1)
    orbitals, me = lax.optimization_barrier((orbitals, me))
    hi, lo = split(orbitals)
    shape = pltpu.VMEM(columns.shape, F32)
    own = pl.pallas_call(
        local_kernel,
        in_specs=[VMEM] * 2,
        out_specs=VMEM,
        out_shape=shape,
        compiler_params=params(),
        name="local",
    )(near(columns), near(potential))
    own, hi, lo = lax.optimization_barrier((own, hi, lo))
    applied = pl.pallas_call(
        halo_kernel,
        in_specs=[VMEM] * 3,
        out_specs=VMEM,
        out_shape=shape,
        compiler_params=params(),
        name="halo",
    )(near(own), near(before), near(after))

    blocks, order = [applied], [0]
    mask = band // 2
    while mask:
        blocks = blocks + [swap(block, "band", mask) for block in blocks]
        order = order + [r ^ mask for r in order]
        mask //= 2
    corr = correlate(hi, lo, blocks)
    steps = [[1, 2, 3]] + [[1 << bit] for bit in range(2, space.bit_length() - 1)]
    parts = [corr]
    for step in steps:
        held = parts[0] if len(parts) == 1 else add(*parts)
        parts = [held] + [swap(held, "space", mask) for mask in step]
    corr, keep, send = remove(order, me, parts, hi, lo, planes, ny, nx)
    mask = 1
    while mask < band:
        kept = keep + swap(send, "band", mask)
        half = kept.shape[0] // 2
        keep, send = kept[:half], kept[half:]
        mask *= 2
    return applied - kept, corr.T


def solution(mesh):
    placed = (
        P("band", "space", None, None),
        P("space", None, None),
        P("band", "space", None, None),
    )
    return jax.shard_map(
        shards,
        mesh=mesh,
        in_specs=placed,
        out_specs=(P("band", "space", None, None), P("band", None)),
        check_vma=False,
    )
```

time: 156 us -> 68.2 us (0.44)
  local copies, waits for them, and re-layouts: 46.5 us -> 7.15 us
  matrix products: 33.4 us -> 0 us
  blocking collectives: 21 us -> 0 us
  between operations: 14.2 us -> 0.7 us
  Pallas kernels: 0 us -> 12.3 us
  starting transfers between devices: 6.41 us -> 14.4 us
  other arithmetic: 5.59 us -> 0.98 us
  waiting for transfers between devices: 28.2 us -> 32.5 us
    dot_general x2 -> x0, matrix products: 33.4 us -> none  [the longest x1 20.7 us: shards(): jnp.einsum('oc,kc->ok', psi_flat, piece.reshape(piece.shape[0], -1), prec...]
    ppermute x2 -> x11, waiting for transfers between devices: 2.73 us -> 32.5 us  [the longest x9 29.6 us: swap(): return lax.ppermute(x, axis, [(i, i ^ mask) for i in range(size)])]
    reduce_scatter x1 -> x0, waiting for transfers between devices: 25.4 us -> none  [shards(): lax.psum_scatter(removed.reshape((col_local * lax.axis_size('band'),) + a...]
    psum x1 -> x0, blocking collectives: 21 us -> none  [shards(): correlation = lax.psum(partial_correlation, 'space')]
    dot_general x2 -> x0, local copies, waits for them, and re-layouts: 14.3 us -> none  [shards(): jnp.einsum('ok,oc->kc', correlation, psi_flat, precision=lax.Precision.HI...]
    slice x24 -> x1, local copies, waits for them, and re-layouts: 13.1 us -> 0.03 us  [shards(): keep, send = (kept[:half], kept[half:])]
    pallas_call x0 -> x6, Pallas kernels: none -> 12.3 us  [the longest x1 3.89 us: split(): pl.pallas_call(split_kernel, grid=(planes * per,), in_specs=[pl.BlockSpec...]
    unnamed x11 -> x7, local copies, waits for them, and re-layouts: 19 us -> 7.12 us
  transfers between devices with their start and end apart: 4 -> 11, of which waited for: 3 -> 10; matrix products, arithmetic and copies ran while one was open for 29% -> 1% of each run, Pallas kernels for 0% -> 8%
where the time goes in v1:
time: 68.2 us; the launch traced here: 68 us
  waiting for transfers between devices  32.5 us (48%)
  starting transfers between devices  14.4 us (21%)
  Pallas kernels  12.3 us (18%)
  local copies, waits for them, and re-layouts  7.15 us (10%)
  other arithmetic  0.98 us (1%)
  between operations  0.7 us (1%)
    ppermute x9, waiting for transfers between devices, swap(): return lax.ppermute(x, axis, [(i, i ^ mask) for i in range(size)])  29.6 us
    ppermute x9, starting transfers between devices, swap(): return lax.ppermute(x, axis, [(i, i ^ mask) for i in range(size)])  8.3 us
    unnamed x7, local copies, waits for them, and re-layouts  7.12 us
    ppermute x1, starting transfers between devices, shards(): after = lax.ppermute(columns[:, :WIDTH], 'space', down)  6.09 us
    pallas_call x1, Pallas kernels, split(): pl.pallas_call(split_kernel, grid=(planes * per,), in_specs=[pl.BlockSpec...  3.89 us
    pallas_call x1, Pallas kernels, correlate(): pl.pallas_call(functools.partial(corr_kernel, len(blocks)), in_specs=[VME...  3.81 us
    pallas_call x1, Pallas kernels, remove(): pl.pallas_call(functools.partial(remove_kernel, order, len(parts)), in_sp...  2.79 us
    ppermute x1, waiting for transfers between devices, shards(): after = lax.ppermute(columns[:, :WIDTH], 'space', down)  2.72 us
  transfers between devices with their start and end apart: 11, of which 10 were waited for; matrix products, arithmetic and copies ran while one was open for 1% of the time, Pallas kernels for 8%

profile of v1, /device:TPU:0, one launch (start us, length us, event | category | flops | bytes accessed | tf_op | source)
XLA Modules:
  0.0 68.0 jit_solution(7472378207239822813)
XLA Ops:
  0.6 6.1 %collective-permute-start.1 = (f32[4,6,32,128]{3,2,1,0:T(8,128)}, f32[4,6,32,128]{3,2,1,0:T(8,128)S(1)}, u32[]{:S(2)}, u32[]{:S(2)}) collective-permute-start(f32[4,6,32,128]{3,2,1,0:T(8,128)} %v_ref.1), channel_id=1, source_target_pairs={{4,0},{8,4},{12,8},{16,12},{20,16},{24,20},{28,24},{0,28},{5,1},{9... | collective-permute-start | bytes 1179656 | tf_op jit(solution)/shard_map/ppermute | solution.py:265
  6.7 0.0 collective-permute-start
  6.7 1.1 %copy-done.1 = f32[4,6,32,128]{3,2,1,0:T(8,128)S(1)} copy-done((f32[4,6,32,128]{3,2,1,0:T(8,128)S(1)}, f32[4,6,32,128]{3,2,1,0:T(8,128)}, u32[]{:S(2)}) %copy-start.1) | copy-done | bytes 393240
  7.8 0.9 %copy-done.2 = f32[6,32,128]{2,1,0:T(8,128)S(1)} copy-done((f32[6,32,128]{2,1,0:T(8,128)S(1)}, f32[6,32,128]{2,1,0:T(8,128)}, u32[]{:S(2)}) %copy-start.2) | copy-done | bytes 98328
  8.7 1.5 %local.1.own_ref = f32[4,6,32,128]{3,2,1,0:T(8,128)S(1)} custom-call(f32[4,6,32,128]{3,2,1,0:T(8,128)S(1)} %copy-done.1, f32[6,32,128]{2,1,0:T(8,128)S(1)} %copy-done.2), custom_call_target="tpu_custom_call" | custom-call | tf_op jit(solution)/shard_map/local/pallas_call | solution.py:270
  10.2 0.0 copy-start
  10.2 4.6 %copy-done = f32[128,6,32,128]{3,2,1,0:T(8,128)S(1)} copy-done((f32[128,6,32,128]{3,2,1,0:T(8,128)S(1)}, f32[128,6,32,128]{3,2,1,0:T(8,128)}, u32[]{:S(2)}) %copy-start) | copy-done | bytes 12582936
  14.8 3.9 %split.1 = (bf16[12,1024,256]{2,1,0:T(8,128)(2,1)S(1)}, bf16[12,1024,256]{2,1,0:T(8,128)(2,1)S(1)}) custom-call(f32[128,6,32,128]{3,2,1,0:T(8,128)S(1)} %copy-done), custom_call_target="tpu_custom_call" | custom-call | flops 12582912 | bytes 25165824 | tf_op jit(solution)/shard_map/split/pallas_call | solution.py:56
  18.7 2.7 %collective-permute-done.1.after_ref = f32[4,6,32,128]{3,2,1,0:T(8,128)S(1)} collective-permute-done((f32[4,6,32,128]{3,2,1,0:T(8,128)}, f32[4,6,32,128]{3,2,1,0:T(8,128)S(1)}, u32[]{:S(2)}, u32[]{:S(2)}) %collective-permute-start.1) | collective-permute-done | bytes 393248 | tf_op jit(solution)/shard_map/ppermute | solution.py:265
  21.4 0.3 collective-permute-done.before_ref
  21.7 0.2 halo.1.refs_0_
  21.9 1.6 %collective-permute-start.2 = (f32[4,6,32,128]{3,2,1,0:T(8,128)S(1)}, f32[4,6,32,128]{3,2,1,0:T(8,128)S(1)}, u32[]{:S(2)}, u32[]{:S(2)}) collective-permute-start(f32[4,6,32,128]{3,2,1,0:T(8,128)S(1)} %halo.1.refs_0_), channel_id=1, source_target_pairs={{0,2},{1,3},{2,0},{3,1},{4,6},{5,7},{6,4},{7,5},{8,10},{9,11},{10,... | collective-permute-start | bytes 1179656 | tf_op jit(solution)/shard_map/ppermute | solution.py:256
  23.5 9.5 %collective-permute-done.2.refs_1_ = f32[4,6,32,128]{3,2,1,0:T(8,128)S(1)} collective-permute-done((f32[4,6,32,128]{3,2,1,0:T(8,128)S(1)}, f32[4,6,32,128]{3,2,1,0:T(8,128)S(1)}, u32[]{:S(2)}, u32[]{:S(2)}) %collective-permute-start.2) | collective-permute-done | bytes 393248 | tf_op jit(solution)/shard_map/ppermute | solution.py:256
  33.0 0.0 collective-permute-start.4
  33.0 1.7 %collective-permute-done.4.refs_3_ = f32[4,6,32,128]{3,2,1,0:T(8,128)S(1)} collective-permute-done((f32[4,6,32,128]{3,2,1,0:T(8,128)S(1)}, f32[4,6,32,128]{3,2,1,0:T(8,128)S(1)}, u32[]{:S(2)}, u32[]{:S(2)}) %collective-permute-start.4) | collective-permute-done | bytes 393248 | tf_op jit(solution)/shard_map/ppermute | solution.py:256
  34.7 3.8 %corr.1.refs_0_ = f32[16,128]{1,0:T(8,128)S(1)} custom-call(bf16[12,1024,256]{2,1,0:T(8,128)(2,1)S(1)} %get-tuple-element.17.hi_ref.refs_2_, bf16[12,1024,256]{2,1,0:T(8,128)(2,1)S(1)} %get-tuple-element.18.lo_ref.refs_3_, f32[4,6,32,128]{3,2,1,0:T(8,128)S(1)} %halo.1.refs_0_, f32[4,6,32,128]{3,2,1,0:T(8,128)S(1)} %collective-permute-done.2.refs_1_, ...), custom_call_target="tpu_custom_call" | custom-call | tf_op jit(solution)/shard_map/corr/pallas_call | solution.py:165
  38.5 2.1 %collective-permute-start.7 = (f32[16,128]{1,0:T(8,128)S(1)}, f32[16,128]{1,0:T(8,128)S(1)}, u32[]{:S(2)}, u32[]{:S(2)}) collective-permute-start(f32[16,128]{1,0:T(8,128)S(1)} %corr.1.refs_0_), channel_id=1, source_target_pairs={{0,12},{4,8},{8,4},{12,0},{16,28},{20,24},{24,20},{28,16},{1,13},{... | collective-permute-start | bytes 24584 | tf_op jit(solution)/shard_map/ppermute | solution.py:256
  40.6 1.8 %collective-permute-start.6 = (f32[16,128]{1,0:T(8,128)S(1)}, f32[16,128]{1,0:T(8,128)S(1)}, u32[]{:S(2)}, u32[]{:S(2)}) collective-permute-start(f32[16,128]{1,0:T(8,128)S(1)} %corr.1.refs_0_), channel_id=1, source_target_pairs={{0,8},{4,12},{8,0},{12,4},{16,24},{20,28},{24,16},{28,20},{1,9},{5... | collective-permute-start | bytes 24584 | tf_op jit(solution)/shard_map/ppermute | solution.py:256
  42.4 0.0 collective-permute-start.5
  42.4 0.7 %collective-permute-done.7.refs_3_ = f32[16,128]{1,0:T(8,128)S(1)} collective-permute-done((f32[16,128]{1,0:T(8,128)S(1)}, f32[16,128]{1,0:T(8,128)S(1)}, u32[]{:S(2)}, u32[]{:S(2)}) %collective-permute-start.7) | collective-permute-done | bytes 8224 | tf_op jit(solution)/shard_map/ppermute | solution.py:256
  43.1 1.1 %collective-permute-done.6.refs_2_ = f32[16,128]{1,0:T(8,128)S(1)} collective-permute-done((f32[16,128]{1,0:T(8,128)S(1)}, f32[16,128]{1,0:T(8,128)S(1)}, u32[]{:S(2)}, u32[]{:S(2)}) %collective-permute-start.6) | collective-permute-done | bytes 8224 | tf_op jit(solution)/shard_map/ppermute | solution.py:256
  44.3 1.8 %collective-permute-done.5.refs_1_ = f32[16,128]{1,0:T(8,128)S(1)} collective-permute-done((f32[16,128]{1,0:T(8,128)S(1)}, f32[16,128]{1,0:T(8,128)S(1)}, u32[]{:S(2)}, u32[]{:S(2)}) %collective-permute-start.5) | collective-permute-done | bytes 8224 | tf_op jit(solution)/shard_map/ppermute | solution.py:256
  46.1 1.2 %collective-permute-start.8 = (f32[16,128]{1,0:T(8,128)S(1)}, f32[16,128]{1,0:T(8,128)S(1)}, u32[]{:S(2)}, u32[]{:S(2)}) collective-permute-start(f32[16,128]{1,0:T(8,128)S(1)} %add.12.refs_0_), channel_id=1, source_target_pairs={{0,16},{4,20},{8,24},{12,28},{16,0},{20,4},{24,8},{28,12},{1,17},{... | collective-permute-start | bytes 24584 | tf_op jit(solution)/shard_map/ppermute | solution.py:256
  47.3 3.3 %collective-permute-done.8.refs_1_ = f32[16,128]{1,0:T(8,128)S(1)} collective-permute-done((f32[16,128]{1,0:T(8,128)S(1)}, f32[16,128]{1,0:T(8,128)S(1)}, u32[]{:S(2)}, u32[]{:S(2)}) %collective-permute-start.8) | collective-permute-done | bytes 8224 | tf_op jit(solution)/shard_map/ppermute | solution.py:256
  50.6 2.8 %remove.1 = (f32[16,128]{1,0:T(8,128)S(1)}, f32[8,6,32,128]{3,2,1,0:T(8,128)S(1)}, f32[8,6,32,128]{3,2,1,0:T(8,128)S(1)}) custom-call(s32[1]{0:T(128)} %bitcast.me_ref, f32[16,128]{1,0:T(8,128)S(1)} %add.12.refs_0_, f32[16,128]{1,0:T(8,128)S(1)} %collective-permute-done.8.refs_1_, bf16[12,1024,256]{2,1,0:T(8,128)(2,1)S(1)} %get-tuple-element.17.hi_ref.refs_2_, ...), custom_call_target="tpu_custom_call" | custom-call | tf_op jit(solution)/shard_map/remove/pallas_call | solution.py:244
  53.4 0.1 collective-permute-start.9
  53.5 2.3 %collective-permute-done.9 = f32[8,6,32,128]{3,2,1,0:T(8,128)S(1)} collective-permute-done((f32[8,6,32,128]{3,2,1,0:T(8,128)S(1)}, f32[8,6,32,128]{3,2,1,0:T(8,128)S(1)}, u32[]{:S(2)}, u32[]{:S(2)}) %collective-permute-start.9) | collective-permute-done | bytes 786464 | tf_op jit(solution)/shard_map/ppermute | solution.py:256
  55.8 0.1 add.7
  56.0 1.6 %collective-permute-start.10 = (f32[4,6,32,128]{3,2,1,0:T(8,128)S(1)}, f32[4,6,32,128]{3,2,1,0:T(8,128)S(1)}, u32[]{:S(2)}, u32[]{:S(2)}) collective-permute-start(f32[4,6,32,128]{3,2,1,0:T(8,128)S(1)} %slice.9), channel_id=1, source_target_pairs={{0,2},{1,3},{2,0},{3,1},{4,6},{5,7},{6,4},{7,5},{8,10},{9,11},{10,... | collective-permute-start | bytes 1179656 | tf_op jit(solution)/shard_map/ppermute | solution.py:256
  57.5 0.6 copy.5
  58.1 9.1 %collective-permute-done.10 = f32[4,6,32,128]{3,2,1,0:T(8,128)S(1)} collective-permute-done((f32[4,6,32,128]{3,2,1,0:T(8,128)S(1)}, f32[4,6,32,128]{3,2,1,0:T(8,128)S(1)}, u32[]{:S(2)}, u32[]{:S(2)}) %collective-permute-start.10) | collective-permute-done | bytes 393248 | tf_op jit(solution)/shard_map/ppermute | solution.py:256
  67.2 0.8 %fusion = f32[4,6,32,128]{3,2,1,0:T(8,128)} fusion(f32[4,6,32,128]{3,2,1,0:T(8,128)S(1)} %halo.1.refs_0_, f32[4,6,32,128]{3,2,1,0:T(8,128)S(1)} %collective-permute-done.10, f32[8,6,32,128]{3,2,1,0:T(8,128)S(1)} %add.7), kind=kLoop, calls=%fused_computation.1 | loop fusion | flops 196608 | bytes 1572864 | tf_op jit(solution)/shard_map/sub | solution.py:307
  (6 shorter events, 0.0 us)
Async XLA Ops:
  0.6 20.8 %collective-permute-start.1 = (f32[4,6,32,128]{3,2,1,0:T(8,128)}, f32[4,6,32,128]{3,2,1,0:T(8,128)S(1)}, u32[]{:S(2)}, u32[]{:S(2)}) collective-permute-start(f32[4,6,32,128]{3,2,1,0:T(8,128)} %v_ref.1), channel_id=1, source_target_pairs={{4,0},{8,4},{12,8},{16,12},{20,16},{24,20},{28,24},{0,28},{5,1},{9... | collective-permute-start | bytes 1179656 | tf_op jit(solution)/shard_map/ppermute | solution.py:265
  6.7 15.0 %collective-permute-start = (f32[4,6,32,128]{3,2,1,0:T(8,128)}, f32[4,6,32,128]{3,2,1,0:T(8,128)S(1)}, u32[]{:S(2)}, u32[]{:S(2)}) collective-permute-start(f32[4,6,32,128]{3,2,1,0:T(8,128)} %v_ref.1), channel_id=1, source_target_pairs={{0,4},{4,8},{8,12},{12,16},{16,20},{20,24},{24,28},{28,0},{1,5},{5... | collective-permute-start | bytes 1179656 | tf_op jit(solution)/shard_map/ppermute | solution.py:264
  6.7 1.1 %copy-start.1 = (f32[4,6,32,128]{3,2,1,0:T(8,128)S(1)}, f32[4,6,32,128]{3,2,1,0:T(8,128)}, u32[]{:S(2)}) copy-start(f32[4,6,32,128]{3,2,1,0:T(8,128)} %v_ref.1) | copy-start | bytes 1179652
  7.8 0.9 %copy-start.2 = (f32[6,32,128]{2,1,0:T(8,128)S(1)}, f32[6,32,128]{2,1,0:T(8,128)}, u32[]{:S(2)}) copy-start(f32[6,32,128]{2,1,0:T(8,128)} %pot_ref.1) | copy-start | bytes 294916
  10.2 4.6 %copy-start = (f32[128,6,32,128]{3,2,1,0:T(8,128)S(1)}, f32[128,6,32,128]{3,2,1,0:T(8,128)}, u32[]{:S(2)}) copy-start(f32[128,6,32,128]{3,2,1,0:T(8,128)} %psi_ref) | copy-start | bytes 37748740
  21.9 11.1 %collective-permute-start.2 = (f32[4,6,32,128]{3,2,1,0:T(8,128)S(1)}, f32[4,6,32,128]{3,2,1,0:T(8,128)S(1)}, u32[]{:S(2)}, u32[]{:S(2)}) collective-permute-start(f32[4,6,32,128]{3,2,1,0:T(8,128)S(1)} %halo.1.refs_0_), channel_id=1, source_target_pairs={{0,2},{1,3},{2,0},{3,1},{4,6},{5,7},{6,4},{7,5},{8,10},{9,11},{10,... | collective-permute-start | bytes 1179656 | tf_op jit(solution)/shard_map/ppermute | solution.py:256
  23.5 9.6 %collective-permute-start.3 = (f32[4,6,32,128]{3,2,1,0:T(8,128)S(1)}, f32[4,6,32,128]{3,2,1,0:T(8,128)S(1)}, u32[]{:S(2)}, u32[]{:S(2)}) collective-permute-start(f32[4,6,32,128]{3,2,1,0:T(8,128)S(1)} %halo.1.refs_0_), channel_id=1, source_target_pairs={{0,1},{1,0},{2,3},{3,2},{4,5},{5,4},{6,7},{7,6},{8,9},{9,8},{10,11... | collective-permute-start | bytes 1179656 | tf_op jit(solution)/shard_map/ppermute | solution.py:256
  33.0 1.7 %collective-permute-start.4 = (f32[4,6,32,128]{3,2,1,0:T(8,128)S(1)}, f32[4,6,32,128]{3,2,1,0:T(8,128)S(1)}, u32[]{:S(2)}, u32[]{:S(2)}) collective-permute-start(f32[4,6,32,128]{3,2,1,0:T(8,128)S(1)} %collective-permute-done.2.refs_1_), channel_id=1, source_target_pairs={{0,1},{1,0},{2,3},{3,2},{4,5},{5,4},{6,7},{7,6},{8,9},{9,8},{10,11... | collective-permute-start | bytes 1179656 | tf_op jit(solution)/shard_map/ppermute | solution.py:256
  38.5 4.6 %collective-permute-start.7 = (f32[16,128]{1,0:T(8,128)S(1)}, f32[16,128]{1,0:T(8,128)S(1)}, u32[]{:S(2)}, u32[]{:S(2)}) collective-permute-start(f32[16,128]{1,0:T(8,128)S(1)} %corr.1.refs_0_), channel_id=1, source_target_pairs={{0,12},{4,8},{8,4},{12,0},{16,28},{20,24},{24,20},{28,16},{1,13},{... | collective-permute-start | bytes 24584 | tf_op jit(solution)/shard_map/ppermute | solution.py:256
  40.6 3.7 %collective-permute-start.6 = (f32[16,128]{1,0:T(8,128)S(1)}, f32[16,128]{1,0:T(8,128)S(1)}, u32[]{:S(2)}, u32[]{:S(2)}) collective-permute-start(f32[16,128]{1,0:T(8,128)S(1)} %corr.1.refs_0_), channel_id=1, source_target_pairs={{0,8},{4,12},{8,0},{12,4},{16,24},{20,28},{24,16},{28,20},{1,9},{5... | collective-permute-start | bytes 24584 | tf_op jit(solution)/shard_map/ppermute | solution.py:256
  42.4 3.7 %collective-permute-start.5 = (f32[16,128]{1,0:T(8,128)S(1)}, f32[16,128]{1,0:T(8,128)S(1)}, u32[]{:S(2)}, u32[]{:S(2)}) collective-permute-start(f32[16,128]{1,0:T(8,128)S(1)} %corr.1.refs_0_), channel_id=1, source_target_pairs={{0,4},{4,0},{8,12},{12,8},{16,20},{20,16},{24,28},{28,24},{1,5},{5... | collective-permute-start | bytes 24584 | tf_op jit(solution)/shard_map/ppermute | solution.py:256
  46.1 4.5 %collective-permute-start.8 = (f32[16,128]{1,0:T(8,128)S(1)}, f32[16,128]{1,0:T(8,128)S(1)}, u32[]{:S(2)}, u32[]{:S(2)}) collective-permute-start(f32[16,128]{1,0:T(8,128)S(1)} %add.12.refs_0_), channel_id=1, source_target_pairs={{0,16},{4,20},{8,24},{12,28},{16,0},{20,4},{24,8},{28,12},{1,17},{... | collective-permute-start | bytes 24584 | tf_op jit(solution)/shard_map/ppermute | solution.py:256
  53.4 2.4 %collective-permute-start.9 = (f32[8,6,32,128]{3,2,1,0:T(8,128)S(1)}, f32[8,6,32,128]{3,2,1,0:T(8,128)S(1)}, u32[]{:S(2)}, u32[]{:S(2)}) collective-permute-start(f32[8,6,32,128]{3,2,1,0:T(8,128)S(1)} %get-tuple-element.20), channel_id=1, source_target_pairs={{0,1},{1,0},{2,3},{3,2},{4,5},{5,4},{6,7},{7,6},{8,9},{9,8},{10,11... | collective-permute-start | bytes 2359304 | tf_op jit(solution)/shard_map/ppermute | solution.py:256
  56.0 11.2 %collective-permute-start.10 = (f32[4,6,32,128]{3,2,1,0:T(8,128)S(1)}, f32[4,6,32,128]{3,2,1,0:T(8,128)S(1)}, u32[]{:S(2)}, u32[]{:S(2)}) collective-permute-start(f32[4,6,32,128]{3,2,1,0:T(8,128)S(1)} %slice.9), channel_id=1, source_target_pairs={{0,2},{1,3},{2,0},{3,1},{4,6},{5,7},{6,4},{7,5},{8,10},{9,11},{10,... | collective-permute-start | bytes 1179656 | tf_op jit(solution)/shard_map/ppermute | solution.py:256

commit v2 on v1

v2 whole, which is shorter than its diff:
```python
import functools

import jax
import jax.numpy as jnp
from jax import lax
from jax.experimental import pallas as pl
from jax.experimental.pallas import tpu as pltpu
from jax.sharding import PartitionSpec as P

COEFFS = (
    -5369.0 / 1800.0,
    12.0 / 7.0,
    -15.0 / 56.0,
    10.0 / 189.0,
    -1.0 / 112.0,
    2.0 / 1925.0,
    -1.0 / 16632.0,
)
WIDTH = 6
SUB = 8
F32 = jnp.float32
BF16 = jnp.bfloat16
VMEM = pl.BlockSpec(memory_space=pltpu.VMEM)
LIMIT = 16 << 20


def near(x):
    return pltpu.with_memory_space_constraint(x, pltpu.VMEM)


def far_off(x):
    return pltpu.with_memory_space_constraint(x, pltpu.HBM)


def params(limit=LIMIT):
    return pltpu.CompilerParams(vmem_limit_bytes=limit)


def halves(x):
    hi = x.astype(BF16)
    lo = (x - hi.astype(F32)).astype(BF16)
    return hi, lo


def cut_kernel(cuts, columns_ref, pot_ref, *refs):
    outs, sems = refs[:-1], refs[-1]
    copies = [pltpu.make_async_copy(pot_ref, outs[-1], sems.at[len(cuts)])]
    copies[0].start()
    for at, (a, b) in enumerate(cuts):
        source = columns_ref.at[pl.ds(a, b - a)]
        copies.append(pltpu.make_async_copy(source, outs[at], sems.at[at]))
        copies[-1].start()
    for copy in copies:
        copy.wait()


def cut(columns, potential, cuts):
    shapes = [(b - a,) + columns.shape[1:] for a, b in cuts] + [potential.shape]
    return pl.pallas_call(
        functools.partial(cut_kernel, cuts),
        in_specs=[pl.BlockSpec(memory_space=pl.ANY)] * 2,
        out_specs=[VMEM] * len(shapes),
        out_shape=[pltpu.VMEM(shape, F32) for shape in shapes],
        scratch_shapes=[pltpu.SemaphoreType.DMA((len(shapes),))],
        compiler_params=params(),
        name="cut",
    )(far_off(columns), far_off(potential))


def split_kernel(first, count, psi_ref, hi_ref, lo_ref, held_ref, sems):
    orbs, planes, ny, lanes = held_ref.shape
    per = ny // (2 * SUB)
    block = orbs // count
    copies = []
    for at in range(count):
        source = psi_ref.at[pl.ds(first + at * block, block)]
        target = held_ref.at[pl.ds(at * block, block)]
        copies.append(pltpu.make_async_copy(source, target, sems.at[at]))
        copies[-1].start()
    for at in range(count):
        copies[at].wait()

        def plane(z, carry):
            for p in range(per):
                for g in range(2):
                    y = (p * 2 + g) * SUB
                    x = held_ref[at * block : (at + 1) * block, z, y : y + SUB, :]
                    hi, lo = halves(x.reshape(block * SUB, lanes))
                    rows = slice(at * block * SUB, (at + 1) * block * SUB)
                    hi_ref[z * per + p, rows, g * lanes : (g + 1) * lanes] = hi
                    lo_ref[z * per + p, rows, g * lanes : (g + 1) * lanes] = lo
            return carry

        lax.fori_loop(0, planes, plane, 0)


def split(orbitals, first, orbs):
    _, planes, ny, nx = orbitals.shape
    count = orbs // 8 if orbs <= 32 else orbs // 16
    shape = pltpu.VMEM((planes * ny // (2 * SUB), orbs * SUB, 2 * nx), BF16)
    return pl.pallas_call(
        functools.partial(split_kernel, first, count),
        in_specs=[pl.BlockSpec(memory_space=pl.ANY)],
        out_specs=[VMEM, VMEM],
        out_shape=[shape, shape],
        scratch_shapes=[
            pltpu.VMEM((orbs, planes, ny, nx), F32),
            pltpu.SemaphoreType.DMA((count,)),
        ],
        compiler_params=params(),
        name="split",
    )(far_off(orbitals))


def local_kernel(pot_ref, *refs):
    half = len(refs) // 2
    for v_ref, out_ref in zip(refs[:half], refs[half:]):
        cols, planes, _, _ = v_ref.shape

        def column(c, carry):
            for z in range(planes):
                v = v_ref[c, z]
                total = (pot_ref[z] - 1.5 * COEFFS[0]) * v
                for k in range(1, WIDTH + 1):
                    along = pltpu.roll(v, k, 1) + pltpu.roll(v, v.shape[1] - k, 1)
                    along = along + pltpu.roll(v, k, 0) + pltpu.roll(v, v.shape[0] - k, 0)
                    if z + k < planes:
                        along = along + v_ref[c, z + k]
                    if z - k >= 0:
                        along = along + v_ref[c, z - k]
                    total = total - (0.5 * COEFFS[k]) * along
                out_ref[c, z] = total
            return carry

        lax.fori_loop(0, cols, column, 0)


def halo_kernel(side_ref, own_ref, one_ref, two_ref, out_ref):
    cols, planes, _, _ = out_ref.shape

    def fill(before_ref, after_ref):
        def column(c, carry):
            for z in range(planes):
                total = own_ref[c, z]
                for k in range(1, WIDTH + 1):
                    if z - k < 0:
                        total = total - (0.5 * COEFFS[k]) * before_ref[c, planes + z - k]
                    if z + k >= planes:
                        total = total - (0.5 * COEFFS[k]) * after_ref[c, z + k - planes]
                out_ref[c, z] = total
            return carry

        lax.fori_loop(0, cols, column, 0)

    @pl.when(side_ref[0] == 0)
    def _():
        fill(two_ref, one_ref)

    @pl.when(side_ref[0] != 0)
    def _():
        fill(one_ref, two_ref)


def rows_of(refs, z, y):
    return jnp.concatenate(
        [
            jnp.concatenate(
                [
                    ref[:, z, y + g * SUB : y + (g + 1) * SUB, :].reshape(
                        ref.shape[0] * SUB, ref.shape[3]
                    )
                    for ref in refs
                ],
                axis=0,
            )
            for g in range(2)
        ],
        axis=1,
    )


def corr_kernel(parts, count, *refs):
    split_refs, blocks = refs[: 2 * parts], refs[2 * parts : 2 * parts + count]
    out_ref = refs[2 * parts + count]
    big_refs, small_refs = refs[-2 * parts : -parts], refs[-parts:]
    planes, ny = blocks[0].shape[1:3]
    per = ny // (2 * SUB)
    width = sum(b.shape[0] for b in blocks) * SUB
    contract = (((1,), (1,)), ((), ()))
    for p in range(planes * per):
        w_hi, w_lo = halves(rows_of(blocks, p // per, (p % per) * 2 * SUB))
        both = jnp.concatenate([w_hi, w_lo], axis=0)
        for part in range(parts):
            hi_ref, lo_ref = split_refs[2 * part : 2 * part + 2]
            big = lax.dot_general(hi_ref[p], both, contract, preferred_element_type=F32)
            small = lax.dot_general(lo_ref[p], w_hi, contract, preferred_element_type=F32)
            if p == 0:
                big_refs[part][...] = big
                small_refs[part][...] = small
            else:
                big_refs[part][...] += big
                small_refs[part][...] += small
    cols = width // SUB
    pick = lax.broadcasted_iota(jnp.int32, (cols, width), 1) // SUB
    pick = pick == lax.broadcasted_iota(jnp.int32, (cols, width), 0)
    diags = []
    for part in range(parts):
        big_ref = big_refs[part]
        total = big_ref[:, :width] + big_ref[:, width:] + small_refs[part][...]
        total = total.reshape(total.shape[0] // SUB, SUB, width)
        at = lax.broadcasted_iota(jnp.int32, total.shape, 1)
        lane = lax.broadcasted_iota(jnp.int32, total.shape, 2)
        diags.append(jnp.sum(jnp.where(lane % SUB == at, total, 0.0), axis=1))
    out_ref[...] = lax.dot_general(
        pick.astype(F32),
        jnp.concatenate(diags, axis=0),
        contract,
        precision=lax.Precision.HIGHEST,
        preferred_element_type=F32,
    )


def correlate(splits, blocks):
    cols = sum(b.shape[0] for b in blocks)
    rows = [hi.shape[1] for hi, _ in splits]
    parts = len(splits)
    flat = [x for pair in splits for x in pair]
    return pl.pallas_call(
        functools.partial(corr_kernel, parts, len(blocks)),
        in_specs=[VMEM] * (len(flat) + len(blocks)),
        out_specs=VMEM,
        out_shape=pltpu.VMEM((cols, sum(rows) // SUB), F32),
        compiler_params=params(),
        scratch_shapes=[pltpu.VMEM((r, 2 * cols * SUB), F32) for r in rows]
        + [pltpu.VMEM((r, cols * SUB), F32) for r in rows],
        name="corr",
    )(*map(near, flat), *map(near, blocks))


def add_kernel(*refs):
    total = refs[0][...]
    for ref in refs[1:-1]:
        total = total + ref[...]
    refs[-1][...] = total


def add(*parts):
    return pl.pallas_call(
        add_kernel,
        in_specs=[VMEM] * len(parts),
        out_specs=VMEM,
        out_shape=pltpu.VMEM(parts[0].shape, F32),
        compiler_params=params(),
        name="add",
    )(*map(near, parts))


def remove_kernel(planes, parts, splits, keep_ref, send_ref):
    parts = [ref[...] for ref in parts]
    cols, orbs = parts[0].shape
    nx = splits[0].shape[2] // 2
    per = keep_ref.shape[2] // (2 * SUB)
    half = keep_ref.shape[0]
    height = cols * SUB
    corr = parts[0]
    for part in parts[1:]:
        corr = corr + part
    tall = jnp.broadcast_to(corr[:, None, :], (cols, SUB, orbs)).reshape(height, orbs)
    tall = halves(tall)
    tables, held = [], 0
    for hi_ref in splits[::2]:
        rows = hi_ref.shape[1]
        at = lax.broadcasted_iota(jnp.int32, (height, rows), 0) % SUB
        same = at == lax.broadcasted_iota(jnp.int32, (height, rows), 1) % SUB
        spread = lax.broadcasted_iota(jnp.int32, (orbs, rows), 1) // SUB + held
        spread = spread == lax.broadcasted_iota(jnp.int32, (orbs, rows), 0)
        spread = spread.astype(BF16)
        picked = [jnp.dot(x, spread, preferred_element_type=F32) for x in tall]
        picked = [jnp.where(same, x, 0.0).astype(BF16) for x in picked]
        tables.append((jnp.concatenate(picked, axis=0), picked[0]))
        held += rows // SUB
    for z in planes:
        for p in range(per):
            total = None
            for (both, c_hi), hi_ref, lo_ref in zip(tables, splits[::2], splits[1::2]):
                big = jnp.dot(both, hi_ref[z * per + p], preferred_element_type=F32)
                small = jnp.dot(c_hi, lo_ref[z * per + p], preferred_element_type=F32)
                some = big[:height] + big[height:] + small
                total = some if total is None else total + some
            y = p * 2 * SUB
            for g in range(2):
                part = total[:, g * nx : (g + 1) * nx].reshape(cols, SUB, nx)
                rows = slice(y + g * SUB, y + (g + 1) * SUB)
                keep_ref[:, z - planes[0], rows, :] = part[:half]
                send_ref[:, z - planes[0], rows, :] = part[half:]
    return corr


def first_kernel(count, planes, *refs):
    remove_kernel(planes, refs[:count], refs[count:-2], *refs[-2:])


def last_kernel(order, count, planes, me_ref, *refs):
    out_ref = refs[-1]
    corr = remove_kernel(planes, refs[:count], refs[count:-3], *refs[-3:-1])
    step = corr.shape[0] // len(order)
    pieces = [None] * len(order)
    for at, r in enumerate(order):
        pieces[r] = corr[at * step : (at + 1) * step]
    mask = 1
    while mask < len(order):
        swap = (me_ref[0] & mask) != 0
        pieces = [jnp.where(swap, pieces[r ^ mask], pieces[r]) for r in range(len(order))]
        mask *= 2
    out_ref[...] = jnp.concatenate(pieces, axis=0)


def remove(parts, splits, planes, ny, nx, order=None, me=None):
    cols, orbs = parts[0].shape
    part = pltpu.VMEM((cols // 2, len(planes), ny, nx), F32)
    flat = [x for pair in splits for x in pair]
    in_specs = [VMEM] * (len(parts) + len(flat))
    args = [*map(near, parts), *map(near, flat)]
    shape = [part, part]
    kernel = functools.partial(first_kernel, len(parts), planes)
    if order is not None:
        in_specs = [pl.BlockSpec(memory_space=pltpu.SMEM)] + in_specs
        args = [me] + args
        shape = shape + [pltpu.VMEM((cols, orbs), F32)]
        kernel = functools.partial(last_kernel, order, len(parts), planes)
    return pl.pallas_call(
        kernel,
        in_specs=in_specs,
        out_specs=[VMEM] * len(shape),
        out_shape=shape,
        compiler_params=params(),
        name="remove",
    )(*args)


def merge_kernel(keep_ref, got_ref, own_ref, send_ref):
    half = own_ref.shape[0]
    own_ref[...] = keep_ref[:half] + got_ref[:half]
    send_ref[...] = keep_ref[half:] + got_ref[half:]


def merge(keep, got):
    half = pltpu.VMEM((keep.shape[0] // 2,) + keep.shape[1:], F32)
    return pl.pallas_call(
        merge_kernel,
        in_specs=[VMEM] * 2,
        out_specs=[VMEM] * 2,
        out_shape=[half, half],
        compiler_params=params(),
        name="merge",
    )(near(keep), near(got))


def finish_kernel(first, count, *refs):
    blocks, kept_ref, got_ref = refs[:count], refs[count], refs[count + 1]
    out_ref, held_ref, sem = refs[-3:]
    planes = kept_ref.shape[1]
    c = 0
    for block in blocks:
        for at in range(block.shape[0]):
            removed = kept_ref[c] + got_ref[c]
            held_ref[c] = block[at, first : first + planes] - removed
            c += 1
    copy = pltpu.make_async_copy(held_ref, out_ref.at[:, pl.ds(first, planes)], sem)
    copy.start()
    copy.wait()


def finish(first, blocks, kept, got, shape, out=None):
    hbm = pl.BlockSpec(memory_space=pl.ANY)
    args = [*map(near, blocks), near(kept), near(got)]
    in_specs = [VMEM] * len(args)
    aliases = {}
    if out is not None:
        aliases = {len(args): 0}
        args, in_specs = args + [out], in_specs + [hbm]
    return pl.pallas_call(
        functools.partial(finish_kernel, first, len(blocks)),
        in_specs=in_specs,
        out_specs=hbm,
        out_shape=jax.ShapeDtypeStruct(shape, F32),
        input_output_aliases=aliases,
        scratch_shapes=[pltpu.VMEM(kept.shape, F32), pltpu.SemaphoreType.DMA],
        compiler_params=params(),
        name="finish",
    )(*args)


def swap(x, axis, mask):
    size = lax.axis_size(axis)
    return lax.ppermute(x, axis, [(i, i ^ mask) for i in range(size)])


def shards(columns, potential, orbitals):
    cols, planes, ny, nx = columns.shape
    space, band = lax.axis_size("space"), lax.axis_size("band")
    even = [(i, i ^ 1) for i in range(space)]
    odd = [(i, (i + 2 * (i % 2) - 1) % space) for i in range(space)]
    cuts = [0, cols // 2, cols // 2 + cols // 4, cols]
    cuts = [(a, b) for a, b in zip(cuts, cuts[1:]) if b > a]
    side = (lax.axis_index("space") & 1).astype(jnp.int32).reshape(1)
    me = lax.axis_index("band").astype(jnp.int32).reshape(1)
    columns, me, side = lax.optimization_barrier((columns, me, side))
    (*pieces, potential), halos = cut(columns, potential, cuts), []
    for piece in pieces:
        one = lax.ppermute(piece, "space", even)
        halos.append((one, lax.ppermute(piece, "space", odd)))
    splits, held = [], 0
    for share in (3, 1):
        some = orbitals.shape[0] * share // 4
        splits.append(split(orbitals, held, some))
        held += some
    own = pl.pallas_call(
        local_kernel,
        in_specs=[VMEM] * (1 + len(cuts)),
        out_specs=[VMEM] * len(cuts),
        out_shape=[pltpu.VMEM(piece.shape, F32) for piece in pieces],
        compiler_params=params(),
        name="local",
    )(near(potential), *map(near, pieces))

    chunks, order = [], [0]
    for at, (one, two) in enumerate(halos):
        chunk = pl.pallas_call(
            halo_kernel,
            in_specs=[pl.BlockSpec(memory_space=pltpu.SMEM)] + [VMEM] * 3,
            out_specs=VMEM,
            out_shape=pltpu.VMEM(two.shape, F32),
            compiler_params=params(),
            name="halo",
        )(side, near(own[at]), near(one), near(two))
        chunks.append([chunk])
    applied = [c[0] for c in chunks]
    mask = band // 2
    while mask:
        for at, c in enumerate(chunks):
            more = []
            for block in c:
                more.append(swap(block, "band", mask))
            chunks[at] = c + more
        order = order + [r ^ mask for r in order]
        mask //= 2
    blocks = [c[at] for at in range(len(order)) for c in chunks]
    corr = correlate(splits, blocks)
    steps = [[1, 2, 3]] + [[1 << bit] for bit in range(2, space.bit_length() - 1)]
    parts = [corr]
    for step in steps:
        held = parts[0] if len(parts) == 1 else add(*parts)
        parts = [held] + [swap(held, "space", mask) for mask in step]

    low, high = tuple(range(planes // 2)), tuple(range(planes // 2, planes))
    keep0, send0 = remove(parts, splits, low, ny, nx)
    keep1, send1, corr = remove(parts, splits, high, ny, nx, order, me)
    out = None
    kept = [(keep0, send0), (keep1, send1)]
    mask = 1
    while mask < band:
        for at, (keep, send) in enumerate(kept):
            got = swap(send, "band", mask)
            if 2 * mask < band:
                kept[at] = merge(keep, got)
            else:
                first = (low, high)[at][0]
                out = finish(first, applied, keep, got, columns.shape, out)
        mask *= 2
    return out, corr.T


def solution(mesh):
    placed = (
        P("band", "space", None, None),
        P("space", None, None),
        P("band", "space", None, None),
    )

    return jax.shard_map(
        shards,
        mesh=mesh,
        in_specs=placed,
        out_specs=(P("band", "space", None, None), P("band", None)),
        check_vma=False,
    )
```

time: 68.2 us -> 69.1 us (1.013)
  starting transfers between devices: 14.4 us -> 25.7 us
  waiting for transfers between devices: 32.5 us -> 24.4 us
  local copies, waits for them, and re-layouts: 7.15 us -> 0.6 us
  Pallas kernels: 12.3 us -> 17.4 us
  other arithmetic: 0.98 us -> 0 us
    ppermute x9 -> x17, waiting for transfers between devices: 29.6 us -> 15.6 us  [swap(): return lax.ppermute(x, axis, [(i, i ^ mask) for i in range(size)])]
    ppermute x2 -> x6, starting transfers between devices: 6.09 us -> 13.6 us  [the longest x3 9.01 us: shards(): halos.append((one, lax.ppermute(piece, 'space', odd)))]
    unnamed x7 -> x1, local copies, waits for them, and re-layouts: 7.12 us -> 0.6 us
    ppermute x2 -> x6, waiting for transfers between devices: 2.98 us -> 8.84 us  [the longest x3 4.42 us: shards(): one = lax.ppermute(piece, 'space', even)]
    pallas_call x5 -> x14, Pallas kernels: 12.2 us -> 17.4 us  [the longest x2 6.09 us: split(): pl.pallas_call(functools.partial(split_kernel, first, count), in_specs=[p...]
    ppermute x9 -> x17, starting transfers between devices: 8.3 us -> 12.1 us  [swap(): return lax.ppermute(x, axis, [(i, i ^ mask) for i in range(size)])]
    sub x1 -> x0, other arithmetic: 0.84 us -> none  [shards(): return (applied - kept, corr.T)]
  transfers between devices with their start and end apart: 11 -> 23, of which waited for: 10 -> 14; matrix products, arithmetic and copies ran while one was open for 1% -> 1% of each run, Pallas kernels for 8% -> 15%
where the time goes in v2:
time: 69.1 us; the launch traced here: 69 us
  starting transfers between devices  25.7 us (37%)
  waiting for transfers between devices  24.4 us (35%)
  Pallas kernels  17.4 us (25%)
  between operations  0.79 us (1%)
    ppermute x17, waiting for transfers between devices, swap(): return lax.ppermute(x, axis, [(i, i ^ mask) for i in range(size)])  15.6 us
    ppermute x17, starting transfers between devices, swap(): return lax.ppermute(x, axis, [(i, i ^ mask) for i in range(size)])  12.1 us
    ppermute x3, starting transfers between devices, shards(): halos.append((one, lax.ppermute(piece, 'space', odd)))  9.01 us
    pallas_call x2, Pallas kernels, split(): pl.pallas_call(functools.partial(split_kernel, first, count), in_specs=[p...  6.09 us
    ppermute x3, starting transfers between devices, shards(): one = lax.ppermute(piece, 'space', even)  4.57 us
    ppermute x3, waiting for transfers between devices, shards(): one = lax.ppermute(piece, 'space', even)  4.42 us
    ppermute x3, waiting for transfers between devices, shards(): halos.append((one, lax.ppermute(piece, 'space', odd)))  4.41 us
    pallas_call x1, Pallas kernels, correlate(): pl.pallas_call(functools.partial(corr_kernel, parts, len(blocks)), in_spe...  3.88 us
  transfers between devices with their start and end apart: 23, of which 14 were waited for; matrix products, arithmetic and copies ran while one was open for 1% of the time, Pallas kernels for 15%

profile of v2, /device:TPU:0, one launch (start us, length us, event | category | flops | bytes accessed | tf_op | source)
XLA Modules:
  0.0 69.0 jit_solution(9802150109157895231)
XLA Ops:
  0.6 1.1 %cut.1 = (f32[2,6,32,128]{3,2,1,0:T(8,128)S(1)}, f32[1,6,32,128]{3,2,1,0:T(8,128)S(1)}, f32[1,6,32,128]{3,2,1,0:T(8,128)S(1)}, f32[6,32,128]{2,1,0:T(8,128)S(1)}) custom-call(f32[4,6,32,128]{3,2,1,0:T(8,128)} %columns_ref, f32[6,32,128]{2,1,0:T(8,128)} %pot_ref.1), custom_call_target="tpu_custom_call" | custom-call | tf_op jit(solution)/shard_map/cut/pallas_call | solution.py:59
  1.8 3.1 %collective-permute-start = (f32[2,6,32,128]{3,2,1,0:T(8,128)S(1)}, f32[2,6,32,128]{3,2,1,0:T(8,128)S(1)}, u32[]{:S(2)}, u32[]{:S(2)}) collective-permute-start(f32[2,6,32,128]{3,2,1,0:T(8,128)S(1)} %get-tuple-element.28.refs_0_), channel_id=1, source_target_pairs={{0,4},{4,0},{8,12},{12,8},{16,20},{20,16},{24,28},{28,24},{1,5},{5... | collective-permute-start | bytes 589832 | tf_op jit(solution)/shard_map/ppermute | solution.py:411
  4.8 3.5 %collective-permute-start.1 = (f32[2,6,32,128]{3,2,1,0:T(8,128)S(1)}, f32[2,6,32,128]{3,2,1,0:T(8,128)S(1)}, u32[]{:S(2)}, u32[]{:S(2)}) collective-permute-start(f32[2,6,32,128]{3,2,1,0:T(8,128)S(1)} %get-tuple-element.28.refs_0_), channel_id=1, source_target_pairs={{0,28},{4,8},{8,4},{12,16},{16,12},{20,24},{24,20},{28,0},{1,29},{... | collective-permute-start | bytes 589832 | tf_op jit(solution)/shard_map/ppermute | solution.py:412
  8.4 1.5 %local.1 = (f32[2,6,32,128]{3,2,1,0:T(8,128)S(1)}, f32[1,6,32,128]{3,2,1,0:T(8,128)S(1)}, f32[1,6,32,128]{3,2,1,0:T(8,128)S(1)}) custom-call(f32[6,32,128]{2,1,0:T(8,128)S(1)} %get-tuple-element.27.pot_ref, f32[2,6,32,128]{3,2,1,0:T(8,128)S(1)} %get-tuple-element.28.refs_0_, f32[1,6,32,128]{3,2,1,0:T(8,128)S(1)} %get-tuple-element.29.refs_1_, ...), custom_call_target="tpu_custom_call" | custom-call | tf_op jit(solution)/shard_map/local/pallas_call | solution.py:418
  9.8 3.4 %collective-permute-done.one_ref = f32[2,6,32,128]{3,2,1,0:T(8,128)S(1)} collective-permute-done((f32[2,6,32,128]{3,2,1,0:T(8,128)S(1)}, f32[2,6,32,128]{3,2,1,0:T(8,128)S(1)}, u32[]{:S(2)}, u32[]{:S(2)}) %collective-permute-start) | collective-permute-done | bytes 196640 | tf_op jit(solution)/shard_map/ppermute | solution.py:411
  13.2 0.7 %collective-permute-done.1.two_ref = f32[2,6,32,128]{3,2,1,0:T(8,128)S(1)} collective-permute-done((f32[2,6,32,128]{3,2,1,0:T(8,128)S(1)}, f32[2,6,32,128]{3,2,1,0:T(8,128)S(1)}, u32[]{:S(2)}, u32[]{:S(2)}) %collective-permute-start.1) | collective-permute-done | bytes 196640 | tf_op jit(solution)/shard_map/ppermute | solution.py:412
  14.1 1.8 %collective-permute-start.6 = (f32[2,6,32,128]{3,2,1,0:T(8,128)S(1)}, f32[2,6,32,128]{3,2,1,0:T(8,128)S(1)}, u32[]{:S(2)}, u32[]{:S(2)}) collective-permute-start(f32[2,6,32,128]{3,2,1,0:T(8,128)S(1)} %halo.3.refs_4_.refs_0_), channel_id=1, source_target_pairs={{0,2},{1,3},{2,0},{3,1},{4,6},{5,7},{6,4},{7,5},{8,10},{9,11},{10,... | collective-permute-start | bytes 589832 | tf_op jit(solution)/shard_map/ppermute | solution.py:396
  15.8 1.5 %collective-permute-start.4 = (f32[1,6,32,128]{3,2,1,0:T(8,128)S(1)}, f32[1,6,32,128]{3,2,1,0:T(8,128)S(1)}, u32[]{:S(2)}, u32[]{:S(2)}) collective-permute-start(f32[1,6,32,128]{3,2,1,0:T(8,128)S(1)} %get-tuple-element.30.refs_2_), channel_id=1, source_target_pairs={{0,4},{4,0},{8,12},{12,8},{16,20},{20,16},{24,28},{28,24},{1,5},{5... | collective-permute-start | bytes 294920 | tf_op jit(solution)/shard_map/ppermute | solution.py:411
  17.3 3.6 %collective-permute-start.5 = (f32[1,6,32,128]{3,2,1,0:T(8,128)S(1)}, f32[1,6,32,128]{3,2,1,0:T(8,128)S(1)}, u32[]{:S(2)}, u32[]{:S(2)}) collective-permute-start(f32[1,6,32,128]{3,2,1,0:T(8,128)S(1)} %get-tuple-element.30.refs_2_), channel_id=1, source_target_pairs={{0,28},{4,8},{8,4},{12,16},{16,12},{20,24},{24,20},{28,0},{1,29},{... | collective-permute-start | bytes 294920 | tf_op jit(solution)/shard_map/ppermute | solution.py:412
  20.9 1.9 %collective-permute-start.3 = (f32[1,6,32,128]{3,2,1,0:T(8,128)S(1)}, f32[1,6,32,128]{3,2,1,0:T(8,128)S(1)}, u32[]{:S(2)}, u32[]{:S(2)}) collective-permute-start(f32[1,6,32,128]{3,2,1,0:T(8,128)S(1)} %get-tuple-element.29.refs_1_), channel_id=1, source_target_pairs={{0,28},{4,8},{8,4},{12,16},{16,12},{20,24},{24,20},{28,0},{1,29},{... | collective-permute-start | bytes 294920 | tf_op jit(solution)/shard_map/ppermute | solution.py:412
  22.8 2.2 %collective-permute-done.5.two_ref = f32[1,6,32,128]{3,2,1,0:T(8,128)S(1)} collective-permute-done((f32[1,6,32,128]{3,2,1,0:T(8,128)S(1)}, f32[1,6,32,128]{3,2,1,0:T(8,128)S(1)}, u32[]{:S(2)}, u32[]{:S(2)}) %collective-permute-start.5) | collective-permute-done | bytes 98336 | tf_op jit(solution)/shard_map/ppermute | solution.py:412
  25.1 0.6 collective-permute-start.8
  25.7 1.1 %collective-permute-done.2.one_ref = f32[1,6,32,128]{3,2,1,0:T(8,128)S(1)} collective-permute-done((f32[1,6,32,128]{3,2,1,0:T(8,128)S(1)}, f32[1,6,32,128]{3,2,1,0:T(8,128)S(1)}, u32[]{:S(2)}, u32[]{:S(2)}) %collective-permute-start.2) | collective-permute-done | bytes 98336 | tf_op jit(solution)/shard_map/ppermute | solution.py:411
  26.8 1.4 %collective-permute-done.3.two_ref = f32[1,6,32,128]{3,2,1,0:T(8,128)S(1)} collective-permute-done((f32[1,6,32,128]{3,2,1,0:T(8,128)S(1)}, f32[1,6,32,128]{3,2,1,0:T(8,128)S(1)}, u32[]{:S(2)}, u32[]{:S(2)}) %collective-permute-start.3) | collective-permute-done | bytes 98336 | tf_op jit(solution)/shard_map/ppermute | solution.py:412
  29.4 1.1 %collective-permute-done.8.refs_9_ = f32[1,6,32,128]{3,2,1,0:T(8,128)S(1)} collective-permute-done((f32[1,6,32,128]{3,2,1,0:T(8,128)S(1)}, f32[1,6,32,128]{3,2,1,0:T(8,128)S(1)}, u32[]{:S(2)}, u32[]{:S(2)}) %collective-permute-start.8) | collective-permute-done | bytes 98336 | tf_op jit(solution)/shard_map/ppermute | solution.py:396
  30.5 2.5 %collective-permute-done.7.refs_8_ = f32[1,6,32,128]{3,2,1,0:T(8,128)S(1)} collective-permute-done((f32[1,6,32,128]{3,2,1,0:T(8,128)S(1)}, f32[1,6,32,128]{3,2,1,0:T(8,128)S(1)}, u32[]{:S(2)}, u32[]{:S(2)}) %collective-permute-start.7) | collective-permute-done | bytes 98336 | tf_op jit(solution)/shard_map/ppermute | solution.py:396
  33.5 4.1 %split.2 = (bf16[12,768,256]{2,1,0:T(8,128)(2,1)S(1)}, bf16[12,768,256]{2,1,0:T(8,128)(2,1)S(1)}) custom-call(f32[128,6,32,128]{3,2,1,0:T(8,128)} %psi_ref.3), custom_call_target="tpu_custom_call" | custom-call | tf_op jit(solution)/shard_map/split/pallas_call | solution.py:101
  37.5 2.0 %split.3 = (bf16[12,256,256]{2,1,0:T(8,128)(2,1)S(1)}, bf16[12,256,256]{2,1,0:T(8,128)(2,1)S(1)}) custom-call(f32[128,6,32,128]{3,2,1,0:T(8,128)} %psi_ref.3), custom_call_target="tpu_custom_call" | custom-call | tf_op jit(solution)/shard_map/split/pallas_call | solution.py:101
  39.6 3.9 %corr.1.refs_0_ = f32[16,128]{1,0:T(8,128)S(1)} custom-call(bf16[12,768,256]{2,1,0:T(8,128)(2,1)S(1)} %get-tuple-element.35.refs_0_.refs_2_, bf16[12,768,256]{2,1,0:T(8,128)(2,1)S(1)} %get-tuple-element.36.refs_1_.refs_3_, bf16[12,256,256]{2,1,0:T(8,128)(2,1)S(1)} %get-tuple-element.37.refs_2_.refs_4_, ...), custom_call_target="tpu_custom_call" | custom-call | tf_op jit(solution)/shard_map/corr/pallas_call | solution.py:228
  44.1 2.9 %collective-permute-start.17 = (f32[16,128]{1,0:T(8,128)S(1)}, f32[16,128]{1,0:T(8,128)S(1)}, u32[]{:S(2)}, u32[]{:S(2)}) collective-permute-start(f32[16,128]{1,0:T(8,128)S(1)} %corr.1.refs_0_), channel_id=1, source_target_pairs={{0,12},{4,8},{8,4},{12,0},{16,28},{20,24},{24,20},{28,16},{1,13},{... | collective-permute-start | bytes 24584 | tf_op jit(solution)/shard_map/ppermute | solution.py:396
  47.5 1.2 %collective-permute-done.17.refs_3_ = f32[16,128]{1,0:T(8,128)S(1)} collective-permute-done((f32[16,128]{1,0:T(8,128)S(1)}, f32[16,128]{1,0:T(8,128)S(1)}, u32[]{:S(2)}, u32[]{:S(2)}) %collective-permute-start.17) | collective-permute-done | bytes 8224 | tf_op jit(solution)/shard_map/ppermute | solution.py:396
  48.8 2.5 %collective-permute-start.18 = (f32[16,128]{1,0:T(8,128)S(1)}, f32[16,128]{1,0:T(8,128)S(1)}, u32[]{:S(2)}, u32[]{:S(2)}) collective-permute-start(f32[16,128]{1,0:T(8,128)S(1)} %add.1.refs_0_), channel_id=1, source_target_pairs={{0,16},{4,20},{8,24},{12,28},{16,0},{20,4},{24,8},{28,12},{1,17},{... | collective-permute-start | bytes 24584 | tf_op jit(solution)/shard_map/ppermute | solution.py:396
  51.3 2.0 %collective-permute-done.18.refs_1_ = f32[16,128]{1,0:T(8,128)S(1)} collective-permute-done((f32[16,128]{1,0:T(8,128)S(1)}, f32[16,128]{1,0:T(8,128)S(1)}, u32[]{:S(2)}, u32[]{:S(2)}) %collective-permute-start.18) | collective-permute-done | bytes 8224 | tf_op jit(solution)/shard_map/ppermute | solution.py:396
  53.3 1.6 %remove.3 = (f32[8,3,32,128]{3,2,1,0:T(8,128)S(1)}, f32[8,3,32,128]{3,2,1,0:T(8,128)S(1)}) custom-call(f32[16,128]{1,0:T(8,128)S(1)} %add.1.refs_0_, f32[16,128]{1,0:T(8,128)S(1)} %collective-permute-done.18.refs_1_, bf16[12,768,256]{2,1,0:T(8,128)(2,1)S(1)} %get-tuple-element.35.refs_0_.refs_2_, ...), custom_call_target="tpu_custom_call" | custom-call | tf_op jit(solution)/shard_map/remove/pallas_call | solution.py:331
  55.0 1.6 %remove.2 = (f32[8,3,32,128]{3,2,1,0:T(8,128)S(1)}, f32[8,3,32,128]{3,2,1,0:T(8,128)S(1)}, f32[16,128]{1,0:T(8,128)S(1)}) custom-call(s32[1]{0:T(128)} %bitcast.me_ref, f32[16,128]{1,0:T(8,128)S(1)} %add.1.refs_0_, f32[16,128]{1,0:T(8,128)S(1)} %collective-permute-done.18.refs_1_, bf16[12,768,256]{2,1,0:T(8,128)(2,1)S(1)} %get-tuple-element.35.refs_0_.refs_2_, ...), custom_call_target="tpu_custom_call" | custom-call | tf_op jit(solution)/shard_map/remove/pallas_call | solution.py:331
  57.1 0.6 collective-permute-start.22
  57.7 0.7 %collective-permute-done.19.got_ref = f32[8,3,32,128]{3,2,1,0:T(8,128)S(1)} collective-permute-done((f32[8,3,32,128]{3,2,1,0:T(8,128)S(1)}, f32[8,3,32,128]{3,2,1,0:T(8,128)S(1)}, u32[]{:S(2)}, u32[]{:S(2)}) %collective-permute-start.19) | collective-permute-done | bytes 393248 | tf_op jit(solution)/shard_map/ppermute | solution.py:396
  58.5 0.9 %collective-permute-start.20 = (f32[4,3,32,128]{3,2,1,0:T(8,128)S(1)}, f32[4,3,32,128]{3,2,1,0:T(8,128)S(1)}, u32[]{:S(2)}, u32[]{:S(2)}) collective-permute-start(f32[4,3,32,128]{3,2,1,0:T(8,128)S(1)} %get-tuple-element.42), channel_id=1, source_target_pairs={{0,2},{1,3},{2,0},{3,1},{4,6},{5,7},{6,4},{7,5},{8,10},{9,11},{10,... | collective-permute-start | bytes 589832 | tf_op jit(solution)/shard_map/ppermute | solution.py:396
  59.9 5.0 %collective-permute-done.22.refs_4_ = f32[4,3,32,128]{3,2,1,0:T(8,128)S(1)} collective-permute-done((f32[4,3,32,128]{3,2,1,0:T(8,128)S(1)}, f32[4,3,32,128]{3,2,1,0:T(8,128)S(1)}, u32[]{:S(2)}, u32[]{:S(2)}) %collective-permute-start.22) | collective-permute-done | bytes 196640 | tf_op jit(solution)/shard_map/ppermute | solution.py:396
  65.0 0.7 %finish.2.refs_5_ = f32[4,6,32,128]{3,2,1,0:T(8,128)} custom-call(f32[2,6,32,128]{3,2,1,0:T(8,128)S(1)} %halo.3.refs_4_.refs_0_, f32[1,6,32,128]{3,2,1,0:T(8,128)S(1)} %halo.4.refs_5_.refs_1_, f32[1,6,32,128]{3,2,1,0:T(8,128)S(1)} %halo.5.refs_6_.refs_2_, f32[4,3,32,128]{3,2,1,0:T(8,128)S(1)} %get-tuple-element.45.refs_3_, ...), custom_call_target="tpu_custom_call" | custom-call | tf_op jit(solution)/shard_map/finish/pallas_call | solution.py:382
  65.7 2.5 %collective-permute-done.20.refs_4_ = f32[4,3,32,128]{3,2,1,0:T(8,128)S(1)} collective-permute-done((f32[4,3,32,128]{3,2,1,0:T(8,128)S(1)}, f32[4,3,32,128]{3,2,1,0:T(8,128)S(1)}, u32[]{:S(2)}, u32[]{:S(2)}) %collective-permute-start.20) | collective-permute-done | bytes 196640 | tf_op jit(solution)/shard_map/ppermute | solution.py:396
  68.2 0.7 %finish.3 = f32[4,6,32,128]{3,2,1,0:T(8,128)} custom-call(f32[2,6,32,128]{3,2,1,0:T(8,128)S(1)} %halo.3.refs_4_.refs_0_, f32[1,6,32,128]{3,2,1,0:T(8,128)S(1)} %halo.4.refs_5_.refs_1_, f32[1,6,32,128]{3,2,1,0:T(8,128)S(1)} %halo.5.refs_6_.refs_2_, f32[4,3,32,128]{3,2,1,0:T(8,128)S(1)} %get-tuple-element.41.refs_3_, ...), custom_call_target="tpu_custom_call", output_to_operand_aliasing={{}: (5, {})} | custom-call | tf_op jit(solution)/shard_map/finish/pallas_call | solution.py:382
  (30 shorter events, 4.3 us)
Async XLA Ops:
  1.8 11.4 %collective-permute-start = (f32[2,6,32,128]{3,2,1,0:T(8,128)S(1)}, f32[2,6,32,128]{3,2,1,0:T(8,128)S(1)}, u32[]{:S(2)}, u32[]{:S(2)}) collective-permute-start(f32[2,6,32,128]{3,2,1,0:T(8,128)S(1)} %get-tuple-element.28.refs_0_), channel_id=1, source_target_pairs={{0,4},{4,0},{8,12},{12,8},{16,20},{20,16},{24,28},{28,24},{1,5},{5... | collective-permute-start | bytes 589832 | tf_op jit(solution)/shard_map/ppermute | solution.py:411
  4.8 9.1 %collective-permute-start.1 = (f32[2,6,32,128]{3,2,1,0:T(8,128)S(1)}, f32[2,6,32,128]{3,2,1,0:T(8,128)S(1)}, u32[]{:S(2)}, u32[]{:S(2)}) collective-permute-start(f32[2,6,32,128]{3,2,1,0:T(8,128)S(1)} %get-tuple-element.28.refs_0_), channel_id=1, source_target_pairs={{0,28},{4,8},{8,4},{12,16},{16,12},{20,24},{24,20},{28,0},{1,29},{... | collective-permute-start | bytes 589832 | tf_op jit(solution)/shard_map/ppermute | solution.py:412
  14.1 15.3 %collective-permute-start.6 = (f32[2,6,32,128]{3,2,1,0:T(8,128)S(1)}, f32[2,6,32,128]{3,2,1,0:T(8,128)S(1)}, u32[]{:S(2)}, u32[]{:S(2)}) collective-permute-start(f32[2,6,32,128]{3,2,1,0:T(8,128)S(1)} %halo.3.refs_4_.refs_0_), channel_id=1, source_target_pairs={{0,2},{1,3},{2,0},{3,1},{4,6},{5,7},{6,4},{7,5},{8,10},{9,11},{10,... | collective-permute-start | bytes 589832 | tf_op jit(solution)/shard_map/ppermute | solution.py:396
  15.8 7.0 %collective-permute-start.4 = (f32[1,6,32,128]{3,2,1,0:T(8,128)S(1)}, f32[1,6,32,128]{3,2,1,0:T(8,128)S(1)}, u32[]{:S(2)}, u32[]{:S(2)}) collective-permute-start(f32[1,6,32,128]{3,2,1,0:T(8,128)S(1)} %get-tuple-element.30.refs_2_), channel_id=1, source_target_pairs={{0,4},{4,0},{8,12},{12,8},{16,20},{20,16},{24,28},{28,24},{1,5},{5... | collective-permute-start | bytes 294920 | tf_op jit(solution)/shard_map/ppermute | solution.py:411
  17.3 7.7 %collective-permute-start.5 = (f32[1,6,32,128]{3,2,1,0:T(8,128)S(1)}, f32[1,6,32,128]{3,2,1,0:T(8,128)S(1)}, u32[]{:S(2)}, u32[]{:S(2)}) collective-permute-start(f32[1,6,32,128]{3,2,1,0:T(8,128)S(1)} %get-tuple-element.30.refs_2_), channel_id=1, source_target_pairs={{0,28},{4,8},{8,4},{12,16},{16,12},{20,24},{24,20},{28,0},{1,29},{... | collective-permute-start | bytes 294920 | tf_op jit(solution)/shard_map/ppermute | solution.py:412
  20.9 5.9 %collective-permute-start.2 = (f32[1,6,32,128]{3,2,1,0:T(8,128)S(1)}, f32[1,6,32,128]{3,2,1,0:T(8,128)S(1)}, u32[]{:S(2)}, u32[]{:S(2)}) collective-permute-start(f32[1,6,32,128]{3,2,1,0:T(8,128)S(1)} %get-tuple-element.29.refs_1_), channel_id=1, source_target_pairs={{0,4},{4,0},{8,12},{12,8},{16,20},{20,16},{24,28},{28,24},{1,5},{5... | collective-permute-start | bytes 294920 | tf_op jit(solution)/shard_map/ppermute | solution.py:411
  20.9 7.3 %collective-permute-start.3 = (f32[1,6,32,128]{3,2,1,0:T(8,128)S(1)}, f32[1,6,32,128]{3,2,1,0:T(8,128)S(1)}, u32[]{:S(2)}, u32[]{:S(2)}) collective-permute-start(f32[1,6,32,128]{3,2,1,0:T(8,128)S(1)} %get-tuple-element.29.refs_1_), channel_id=1, source_target_pairs={{0,28},{4,8},{8,4},{12,16},{16,12},{20,24},{24,20},{28,0},{1,29},{... | collective-permute-start | bytes 294920 | tf_op jit(solution)/shard_map/ppermute | solution.py:412
  25.1 5.4 %collective-permute-start.8 = (f32[1,6,32,128]{3,2,1,0:T(8,128)S(1)}, f32[1,6,32,128]{3,2,1,0:T(8,128)S(1)}, u32[]{:S(2)}, u32[]{:S(2)}) collective-permute-start(f32[1,6,32,128]{3,2,1,0:T(8,128)S(1)} %halo.5.refs_6_.refs_2_), channel_id=1, source_target_pairs={{0,2},{1,3},{2,0},{3,1},{4,6},{5,7},{6,4},{7,5},{8,10},{9,11},{10,... | collective-permute-start | bytes 294920 | tf_op jit(solution)/shard_map/ppermute | solution.py:396
  28.3 4.7 %collective-permute-start.7 = (f32[1,6,32,128]{3,2,1,0:T(8,128)S(1)}, f32[1,6,32,128]{3,2,1,0:T(8,128)S(1)}, u32[]{:S(2)}, u32[]{:S(2)}) collective-permute-start(f32[1,6,32,128]{3,2,1,0:T(8,128)S(1)} %halo.4.refs_5_.refs_1_), channel_id=1, source_target_pairs={{0,2},{1,3},{2,0},{3,1},{4,6},{5,7},{6,4},{7,5},{8,10},{9,11},{10,... | collective-permute-start | bytes 294920 | tf_op jit(solution)/shard_map/ppermute | solution.py:396
  28.9 4.1 %collective-permute-start.11 = (f32[1,6,32,128]{3,2,1,0:T(8,128)S(1)}, f32[1,6,32,128]{3,2,1,0:T(8,128)S(1)}, u32[]{:S(2)}, u32[]{:S(2)}) collective-permute-start(f32[1,6,32,128]{3,2,1,0:T(8,128)S(1)} %halo.5.refs_6_.refs_2_), channel_id=1, source_target_pairs={{0,1},{1,0},{2,3},{3,2},{4,5},{5,4},{6,7},{7,6},{8,9},{9,8},{10,11... | collective-permute-start | bytes 294920 | tf_op jit(solution)/shard_map/ppermute | solution.py:396
  28.9 10.7 %collective-permute-start.9 = (f32[2,6,32,128]{3,2,1,0:T(8,128)S(1)}, f32[2,6,32,128]{3,2,1,0:T(8,128)S(1)}, u32[]{:S(2)}, u32[]{:S(2)}) collective-permute-start(f32[2,6,32,128]{3,2,1,0:T(8,128)S(1)} %halo.3.refs_4_.refs_0_), channel_id=1, source_target_pairs={{0,1},{1,0},{2,3},{3,2},{4,5},{5,4},{6,7},{7,6},{8,9},{9,8},{10,11... | collective-permute-start | bytes 589832 | tf_op jit(solution)/shard_map/ppermute | solution.py:396
  29.4 10.2 %collective-permute-start.12 = (f32[2,6,32,128]{3,2,1,0:T(8,128)S(1)}, f32[2,6,32,128]{3,2,1,0:T(8,128)S(1)}, u32[]{:S(2)}, u32[]{:S(2)}) collective-permute-start(f32[2,6,32,128]{3,2,1,0:T(8,128)S(1)} %collective-permute-done.6.refs_7_), channel_id=1, source_target_pairs={{0,1},{1,0},{2,3},{3,2},{4,5},{5,4},{6,7},{7,6},{8,9},{9,8},{10,11... | collective-permute-start | bytes 589832 | tf_op jit(solution)/shard_map/ppermute | solution.py:396
  30.5 9.1 %collective-permute-start.10 = (f32[1,6,32,128]{3,2,1,0:T(8,128)S(1)}, f32[1,6,32,128]{3,2,1,0:T(8,128)S(1)}, u32[]{:S(2)}, u32[]{:S(2)}) collective-permute-start(f32[1,6,32,128]{3,2,1,0:T(8,128)S(1)} %halo.4.refs_5_.refs_1_), channel_id=1, source_target_pairs={{0,1},{1,0},{2,3},{3,2},{4,5},{5,4},{6,7},{7,6},{8,9},{9,8},{10,11... | collective-permute-start | bytes 294920 | tf_op jit(solution)/shard_map/ppermute | solution.py:396
  33.0 6.6 %collective-permute-start.14 = (f32[1,6,32,128]{3,2,1,0:T(8,128)S(1)}, f32[1,6,32,128]{3,2,1,0:T(8,128)S(1)}, u32[]{:S(2)}, u32[]{:S(2)}) collective-permute-start(f32[1,6,32,128]{3,2,1,0:T(8,128)S(1)} %collective-permute-done.8.refs_9_), channel_id=1, source_target_pairs={{0,1},{1,0},{2,3},{3,2},{4,5},{5,4},{6,7},{7,6},{8,9},{9,8},{10,11... | collective-permute-start | bytes 294920 | tf_op jit(solution)/shard_map/ppermute | solution.py:396
  33.0 6.6 %collective-permute-start.13 = (f32[1,6,32,128]{3,2,1,0:T(8,128)S(1)}, f32[1,6,32,128]{3,2,1,0:T(8,128)S(1)}, u32[]{:S(2)}, u32[]{:S(2)}) collective-permute-start(f32[1,6,32,128]{3,2,1,0:T(8,128)S(1)} %collective-permute-done.7.refs_8_), channel_id=1, source_target_pairs={{0,1},{1,0},{2,3},{3,2},{4,5},{5,4},{6,7},{7,6},{8,9},{9,8},{10,11... | collective-permute-start | bytes 294920 | tf_op jit(solution)/shard_map/ppermute | solution.py:396
  43.5 3.7 %collective-permute-start.15 = (f32[16,128]{1,0:T(8,128)S(1)}, f32[16,128]{1,0:T(8,128)S(1)}, u32[]{:S(2)}, u32[]{:S(2)}) collective-permute-start(f32[16,128]{1,0:T(8,128)S(1)} %corr.1.refs_0_), channel_id=1, source_target_pairs={{0,4},{4,0},{8,12},{12,8},{16,20},{20,16},{24,28},{28,24},{1,5},{5... | collective-permute-start | bytes 24584 | tf_op jit(solution)/shard_map/ppermute | solution.py:396
  43.8 3.7 %collective-permute-start.16 = (f32[16,128]{1,0:T(8,128)S(1)}, f32[16,128]{1,0:T(8,128)S(1)}, u32[]{:S(2)}, u32[]{:S(2)}) collective-permute-start(f32[16,128]{1,0:T(8,128)S(1)} %corr.1.refs_0_), channel_id=1, source_target_pairs={{0,8},{4,12},{8,0},{12,4},{16,24},{20,28},{24,16},{28,20},{1,9},{5... | collective-permute-start | bytes 24584 | tf_op jit(solution)/shard_map/ppermute | solution.py:396
  44.1 4.6 %collective-permute-start.17 = (f32[16,128]{1,0:T(8,128)S(1)}, f32[16,128]{1,0:T(8,128)S(1)}, u32[]{:S(2)}, u32[]{:S(2)}) collective-permute-start(f32[16,128]{1,0:T(8,128)S(1)} %corr.1.refs_0_), channel_id=1, source_target_pairs={{0,12},{4,8},{8,4},{12,0},{16,28},{20,24},{24,20},{28,16},{1,13},{... | collective-permute-start | bytes 24584 | tf_op jit(solution)/shard_map/ppermute | solution.py:396
  48.8 4.5 %collective-permute-start.18 = (f32[16,128]{1,0:T(8,128)S(1)}, f32[16,128]{1,0:T(8,128)S(1)}, u32[]{:S(2)}, u32[]{:S(2)}) collective-permute-start(f32[16,128]{1,0:T(8,128)S(1)} %add.1.refs_0_), channel_id=1, source_target_pairs={{0,16},{4,20},{8,24},{12,28},{16,0},{20,4},{24,8},{28,12},{1,17},{... | collective-permute-start | bytes 24584 | tf_op jit(solution)/shard_map/ppermute | solution.py:396
  54.9 2.2 %collective-permute-start.21 = (f32[8,3,32,128]{3,2,1,0:T(8,128)S(1)}, f32[8,3,32,128]{3,2,1,0:T(8,128)S(1)}, u32[]{:S(2)}, u32[]{:S(2)}) collective-permute-start(f32[8,3,32,128]{3,2,1,0:T(8,128)S(1)} %get-tuple-element.44), channel_id=1, source_target_pairs={{0,1},{1,0},{2,3},{3,2},{4,5},{5,4},{6,7},{7,6},{8,9},{9,8},{10,11... | collective-permute-start | bytes 1179656 | tf_op jit(solution)/shard_map/ppermute | solution.py:396
  56.5 1.9 %collective-permute-start.19 = (f32[8,3,32,128]{3,2,1,0:T(8,128)S(1)}, f32[8,3,32,128]{3,2,1,0:T(8,128)S(1)}, u32[]{:S(2)}, u32[]{:S(2)}) collective-permute-start(f32[8,3,32,128]{3,2,1,0:T(8,128)S(1)} %get-tuple-element.40), channel_id=1, source_target_pairs={{0,1},{1,0},{2,3},{3,2},{4,5},{5,4},{6,7},{7,6},{8,9},{9,8},{10,11... | collective-permute-start | bytes 1179656 | tf_op jit(solution)/shard_map/ppermute | solution.py:396
  57.1 7.8 %collective-permute-start.22 = (f32[4,3,32,128]{3,2,1,0:T(8,128)S(1)}, f32[4,3,32,128]{3,2,1,0:T(8,128)S(1)}, u32[]{:S(2)}, u32[]{:S(2)}) collective-permute-start(f32[4,3,32,128]{3,2,1,0:T(8,128)S(1)} %get-tuple-element.46), channel_id=1, source_target_pairs={{0,2},{1,3},{2,0},{3,1},{4,6},{5,7},{6,4},{7,5},{8,10},{9,11},{10,... | collective-permute-start | bytes 589832 | tf_op jit(solution)/shard_map/ppermute | solution.py:396
  58.5 9.8 %collective-permute-start.20 = (f32[4,3,32,128]{3,2,1,0:T(8,128)S(1)}, f32[4,3,32,128]{3,2,1,0:T(8,128)S(1)}, u32[]{:S(2)}, u32[]{:S(2)}) collective-permute-start(f32[4,3,32,128]{3,2,1,0:T(8,128)S(1)} %get-tuple-element.42), channel_id=1, source_target_pairs={{0,2},{1,3},{2,0},{3,1},{4,6},{5,7},{6,4},{7,5},{8,10},{9,11},{10,... | collective-permute-start | bytes 589832 | tf_op jit(solution)/shard_map/ppermute | solution.py:396
